TPU v7x, 512 devices: a whole 4x8x8 slice. The times are simulated.
512 devices in a mesh: build: 128 (over z, y, core), prop: 4 (over x).
Axes of the slice: x: 4, y: 8, z: 8, core: 2. Of those that a mesh axis runs over, the one named last changes fastest.
Arguments:
- cholesky: bfloat16 [48, 2048, 2048], P(None, 'build'), may hold values from -0.09375 to 0.09375
- half_vectors: bfloat16 [48, 2048, 128], P(None, 'build'), may hold values from -0.00390625 to 0.00390625
- walkers: bfloat16 [512, 2048, 128], P(('build', 'prop')), may hold values from -6 to 6
- inverse_intersection: bfloat16 [512, 128, 128], P(('build', 'prop')), may hold values from -1.5 to 2.5
- fields: float32 [512, 48], replicated, may hold values from -6 to 6
- weights: float32 [512], replicated, may hold values from 0.5 to 2
- sources: int32 [512], replicated, may hold values from 0 to 511, as said below
Outputs:
- new_walkers: bfloat16 [512, 2048, 128], P(('build', 'prop'))
- new_weights: float32 [512], P(('build', 'prop'))
Inputs may be any that keep to these rules, and one draw needn't show every extreme that they name: sources[w] has the same remainder modulo 4 as w; walkers 0 and 511 continue their own states.
All inputs are finite; a program needn't handle non-finite values.
Results may differ from a plain program's by a relative error of at most 0.014.
Values may be sent and summed in bfloat16 or wider, within the bound.
No kernel may reach another device: no remote copies, remote signals or barrier semaphores. Data moves between devices by JAX's collectives and lax.ppermute only.
A program may use at most 64 MiB of HBM per device.

v0:
```python
import jax
import jax.numpy as jnp
from jax import lax
from jax.sharding import Mesh
from jax.sharding import PartitionSpec as P

ORDER = 6
BUILD = ("build_0", "build_1", "build_2")
BUILD_PROP = ("build_0", "build_1", "build_2", "prop")


def sent_together(arrays, axis, split_dim, concat_dim, along):
    both = jnp.concatenate(arrays, axis=along)
    result, at, gathered = (
        lax.all_to_all(both, axis, split_axis=split_dim, concat_axis=concat_dim, tiled=True),
        0,
        [],
    )
    for a in arrays:
        gathered.append(lax.slice_in_dim(result, at, at + a.shape[along], axis=along))
        at += a.shape[along]
    return tuple(gathered)


def by_axis(value, axes):
    for axis in axes:
        value = lax.psum(value, axis)
    return value


def sent_to_all(value, axis):
    copies = jnp.broadcast_to(value, (lax.axis_size(axis), *value.shape))
    return lax.all_to_all(copies, axis, split_axis=0, concat_axis=0, tiled=True)


def of_everyone(value, axis):
    everything = sent_to_all(value, axis)
    return jnp.sum(everything, axis=0)


def series(potential, begin_state):
    summed = begin_state.astype(jnp.float32)
    current = begin_state
    for degree in range(1, ORDER + 1):
        product = jnp.dot(potential, current, preferred_element_type=jnp.float32) / degree
        summed = summed + product
        current = product.astype(jnp.bfloat16)
    return summed.astype(jnp.bfloat16)


def factors(force_bias, chosen_fields, chosen_weights):
    exponent = jnp.sum(force_bias * (chosen_fields - 0.5 * force_bias), axis=-1)
    return chosen_weights * jnp.exp(exponent)


def shards(cholesky, half_vectors, walkers, inverse_intersection, fields, weights, sources):
    build_count = lax.axis_size(BUILD)
    prop_count = lax.axis_size("prop")
    builder = lax.axis_index(BUILD)
    member = lax.axis_index("prop")
    orbitals = walkers.shape[1]
    electrons = walkers.shape[2]
    vectors = cholesky.shape[0]
    block_rows = orbitals // build_count
    own_state = walkers[0]
    theta_full = jnp.dot(
        own_state, inverse_intersection[0], preferred_element_type=jnp.float32
    ).astype(jnp.bfloat16)
    outgoing = (
        theta_full.reshape(1, build_count, block_rows, electrons),
        own_state.reshape(1, build_count, block_rows, electrons),
    )
    got_theta, got_state = sent_together((outgoing[0], outgoing[1]), BUILD, 1, 0, 2)
    partial_value = jnp.einsum(
        "wri,gri->wg", got_theta[:, 0], half_vectors, preferred_element_type=jnp.float32
    )
    force_bias = by_axis(partial_value, BUILD)
    group_fields = lax.dynamic_index_in_dim(
        fields.reshape(build_count, prop_count, vectors), member, 1, False
    )
    group_weights = lax.dynamic_index_in_dim(
        weights.reshape(build_count, prop_count), member, 1, False
    )
    group_sources = (
        lax.dynamic_index_in_dim(sources.reshape(build_count, prop_count), member, 1, False)
        // prop_count
    )
    grown_weights = factors(force_bias, group_fields, group_weights)
    overall = of_everyone(jnp.sum(grown_weights), "prop")
    coeffs = (group_fields - force_bias).astype(jnp.bfloat16)
    picked = jnp.take(coeffs, group_sources, axis=0)
    pot_tiles = jnp.dot(
        picked, cholesky.reshape(vectors, block_rows * orbitals), preferred_element_type=jnp.float32
    )
    pot_tiles = pot_tiles.astype(jnp.bfloat16).reshape(build_count, 1, block_rows, orbitals)
    starts = jnp.take(got_state, group_sources, axis=0)
    potential, begin_state = sent_together((pot_tiles, starts), BUILD, 0, 1, 3)
    own_source = lax.dynamic_index_in_dim(group_sources, builder, 0, False)
    kept_weight = lax.dynamic_index_in_dim(grown_weights, own_source, 0, False)
    stepped = series(
        potential.reshape(orbitals, orbitals), begin_state.reshape(orbitals, electrons)
    )
    new_weight = kept_weight * (build_count * prop_count) / overall
    return (stepped[None], new_weight.reshape(1))


def solution(mesh):
    torus = Mesh(
        mesh.devices.reshape(8, 8, 2, mesh.shape["prop"]), ("build_0", "build_1", "build_2", "prop")
    )
    return jax.shard_map(
        shards,
        mesh=torus,
        in_specs=(
            P(None, BUILD, None),
            P(None, BUILD, None),
            P(BUILD_PROP, None, None),
            P(BUILD_PROP, None, None),
            P(),
            P(),
            P(),
        ),
        out_specs=(P(BUILD_PROP, None, None), P(BUILD_PROP)),
        check_vma=False,
    )
```

profile of v0, /device:TPU:28, one launch (start us, length us, event | category | flops | bytes accessed | tf_op | source)
XLA Modules:
  0.0 450.6 jit_solution(8121696317628718935)
XLA Ops:
  0.6 1.4 convolution_convert_fusion.1
  2.0 2.2 maximum_bitcast_fusion
  4.2 17.6 %all-to-all-start = ((bf16[1,128,32,128]{3,2,0,1:T(8,128)(2,1)}), bf16[1,128,32,128]{3,2,0,1:T(8,128)(2,1)}, u32[]{:S(2)}, u32[]{:S(2)}) async-start(bf16[1,128,32,128]{3,2,0,1:T(8,128)(2,1)} %maximum_bitcast_fusion), calls=%async_computation | async-start | bytes 2097152 | tf_op jit(solution)/shard_map/all_to_all | solution.py:15
  24.9 3.7 copy.57
  28.7 22.5 %all-to-all-done = bf16[1,128,32,128]{3,2,0,1:T(8,128)(2,1)} async-done(((bf16[1,128,32,128]{3,2,0,1:T(8,128)(2,1)}), bf16[1,128,32,128]{3,2,0,1:T(8,128)(2,1)}, u32[]{:S(2)}, u32[]{:S(2)}) %all-to-all-start) | async-done | bytes 1048608 | tf_op jit(solution)/shard_map/all_to_all | solution.py:15
  51.2 1.6 copy.62
  54.3 28.2 %psum.21 = f32[128,48]{0,1:T(8,128)S(1)} all-reduce(f32[128,48]{0,1:T(8,128)S(1)} %convolution_bitcast_fusion), channel_id=1, replica_groups=mesh['build_0'=8,'build_1'=8,'build_2'=2,'prop'=4] {'build_0'}, use_global_device_ids=true, to_apply=%region_0.0 | all-reduce | flops 6144 | bytes 49152 | tf_op jit(solution)/shard_map/psum | solution.py:27
  82.6 26.6 %psum.22 = f32[128,48]{0,1:T(8,128)S(1)} all-reduce(f32[128,48]{0,1:T(8,128)S(1)} %psum.21), channel_id=1, replica_groups=mesh['build_0'=8,'build_1'=8,'build_2'=2,'prop'=4] {'build_1'}, use_global_device_ids=true, to_apply=%region_1.0 | all-reduce | flops 6144 | bytes 49152 | tf_op jit(solution)/shard_map/psum | solution.py:27
  109.2 3.4 psum.23
  114.5 4.8 %all-to-all-start.2 = ((f32[4,1,1]{2,1,0:T(1,128)}), f32[4,1,1]{2,1,0:T(1,128)S(1)}, u32[]{:S(2)}, u32[]{:S(2)}) async-start(f32[4,1,1]{2,1,0:T(1,128)} %broadcast_in_dim.31), calls=%async_computation.2 | async-start | bytes 4096 | tf_op jit(solution)/shard_map/all_to_all | solution.py:33
  119.4 2.5 gather_fusion.1
  122.6 2.0 fusion.3
  124.7 5.6 %convolution_convert_fusion = bf16[128,32768]{1,0:T(8,128)(2,1)} fusion(bf16[48,32768]{1,0:T(8,128)(2,1)S(1)} %bitcast.68, bf16[128,48]{1,0:T(8,128)(2,1)S(1)} %gather_fusion, pred[128]{0:T(512)(128)(4,1)S(1)} %get-tuple-element.4), kind=kOutput, calls=%fused_computation.2 | convolution fusion | flops 406853632 | bytes 11546752 | tf_op jit(solution)/shard_map/dot_general | solution.py:92
  130.3 13.0 %copy.58 = bf16[16,8,16,2048]{3,2,1,0:T(8,128)(2,1)} copy(bf16[16,8,16,2048]{3,1,2,0:T(8,128)(2,1)} %bitcast.66) | data formatting | bytes 16777216
  143.3 7.9 %pad_maximum_fusion = bf16[128,1,16,2176]{3,2,1,0:T(8,128)(2,1)} fusion(bf16[128,1,16,128]{3,2,1,0:T(8,128)(2,1)S(1)} %copy-done.2, bf16[128,1,16,2048]{3,2,1,0:T(8,128)(2,1)} %bitcast.67), kind=kLoop, calls=%fused_computation.3 | loop fusion | flops 17825792 | bytes 17825792 | tf_op jit(solution)/shard_map/concatenate | solution.py:13
  151.1 11.8 %all-to-all-start.1 = ((bf16[128,1,16,2176]{3,2,1,0:T(8,128)(2,1)}), bf16[128,1,16,2176]{3,2,1,0:T(8,128)(2,1)}, u32[]{:S(2)}, u32[]{:S(2)}) async-start(bf16[128,1,16,2176]{3,2,1,0:T(8,128)(2,1)} %pad_maximum_fusion), calls=%async_computation.1 | async-start | bytes 17825792 | tf_op jit(solution)/shard_map/all_to_all | solution.py:15
  168.2 253.1 %all-to-all-done.1 = bf16[128,1,16,2176]{3,2,1,0:T(8,128)(2,1)} async-done(((bf16[128,1,16,2176]{3,2,1,0:T(8,128)(2,1)}), bf16[128,1,16,2176]{3,2,1,0:T(8,128)(2,1)}, u32[]{:S(2)}, u32[]{:S(2)}) %all-to-all-start.1) | async-done | bytes 8912928 | tf_op jit(solution)/shard_map/all_to_all | solution.py:15
  422.4 8.3 %slice.23 = bf16[1,128,16,2048]{3,2,1,0:T(8,128)(2,1)} slice(bf16[1,128,16,2176]{3,2,1,0:T(8,128)(2,1)} %bitcast.14), slice={[0:1], [0:128], [0:16], [0:2048]} | slice | bytes 16777216 | tf_op jit(solution)/shard_map/slice | solution.py:20
  430.6 5.9 %fusion.22 = f32[2048,128]{1,0:T(8,128)S(1)} fusion(bf16[2048,2048]{1,0:T(8,128)(2,1)} %bitcast.60, bf16[2048,128]{1,0:T(8,128)(2,1)S(1)} %bitcast.70), kind=kOutput, calls=%fused_computation.56 | convolution fusion | flops 1073741824 | bytes 9961472 | tf_op jit(solution)/shard_map/dot_general | solution.py:45
  436.6 2.4 convolution_multiply_fusion.4
  439.0 2.4 convolution_multiply_fusion.3
  441.3 2.4 convolution_multiply_fusion.2
  443.7 2.4 convolution_multiply_fusion.1
  446.1 3.4 fusion.2
  (30 shorter events, 10.4 us)
Async XLA Ops:
  0.6 52.3 %copy-start = (bf16[48,16,128]{2,1,0:T(8,128)(2,1)S(1)}, bf16[48,16,128]{2,1,0:T(8,128)(2,1)}, u32[]{:S(2)}) copy-start(bf16[48,16,128]{2,1,0:T(8,128)(2,1)} %param.8) | copy-start | bytes 589828
  4.2 47.0 %all-to-all-start = ((bf16[1,128,32,128]{3,2,0,1:T(8,128)(2,1)}), bf16[1,128,32,128]{3,2,0,1:T(8,128)(2,1)}, u32[]{:S(2)}, u32[]{:S(2)}) async-start(bf16[1,128,32,128]{3,2,0,1:T(8,128)(2,1)} %maximum_bitcast_fusion), calls=%async_computation | async-start | bytes 2097152 | tf_op jit(solution)/shard_map/all_to_all | solution.py:15
  114.5 36.6 %all-to-all-start.2 = ((f32[4,1,1]{2,1,0:T(1,128)}), f32[4,1,1]{2,1,0:T(1,128)S(1)}, u32[]{:S(2)}, u32[]{:S(2)}) async-start(f32[4,1,1]{2,1,0:T(1,128)} %broadcast_in_dim.31), calls=%async_computation.2 | async-start | bytes 4096 | tf_op jit(solution)/shard_map/all_to_all | solution.py:33
  130.3 13.0 %copy-start.2 = (bf16[128,1,16,128]{3,2,1,0:T(8,128)(2,1)S(1)}, bf16[128,1,16,128]{3,2,1,0:T(8,128)(2,1)}, u32[]{:S(2)}) copy-start(bf16[128,1,16,128]{3,2,1,0:T(8,128)(2,1)} %fusion.3) | copy-start | bytes 1572868
  151.1 270.2 %all-to-all-start.1 = ((bf16[128,1,16,2176]{3,2,1,0:T(8,128)(2,1)}), bf16[128,1,16,2176]{3,2,1,0:T(8,128)(2,1)}, u32[]{:S(2)}, u32[]{:S(2)}) async-start(bf16[128,1,16,2176]{3,2,1,0:T(8,128)(2,1)} %pad_maximum_fusion), calls=%async_computation.1 | async-start | bytes 17825792 | tf_op jit(solution)/shard_map/all_to_all | solution.py:15
  430.6 5.9 %copy-start.1 = (bf16[1,128,16,2048]{3,2,1,0:T(8,128)(2,1)S(1)}, bf16[1,128,16,2048]{3,2,1,0:T(8,128)(2,1)}, u32[]{:S(2)}) copy-start(bf16[1,128,16,2048]{3,2,1,0:T(8,128)(2,1)} %slice.23) | copy-start | bytes 25165828
where the time goes:
time: 451 us
  waiting for transfers between devices  276 us (61%)
  blocking collectives  58.3 us (13%)
  local copies, waits for them, and re-layouts  37.6 us (8%)
  starting transfers between devices  34.2 us (8%)
  matrix products  26 us (6%)
  other arithmetic  13.6 us (3%)
  between operations  5.24 us (1%)
    all_to_all x2, waiting for transfers between devices, sent_together(): lax.all_to_all(both, axis, split_axis=split_dim, concat_axis=concat_dim,...  276 us
    psum x3, blocking collectives, by_axis(): value = lax.psum(value, axis)  58.3 us
    all_to_all x2, starting transfers between devices, sent_together(): lax.all_to_all(both, axis, split_axis=split_dim, concat_axis=concat_dim,...  29.4 us
    dot_general x6, matrix products, series(): jnp.dot(potential, current, preferred_element_type=jnp.float32) / degree  18.8 us
    unnamed x9, local copies, waits for them, and re-layouts  17.6 us
    slice x4, local copies, waits for them, and re-layouts, sent_together(): lax.slice_in_dim(result, at, at + a.shape[along], axis=along)  10.5 us
    concatenate x2, other arithmetic, sent_together(): both = jnp.concatenate(arrays, axis=along)  10 us
  transfers between devices with their start and end apart: 3, of which 2 were waited for; matrix products, arithmetic and copies ran while one was open for 9% of the time, Pallas kernels for 0%

commit v1 on v0

v1 whole, which is shorter than its diff:
```python
import functools

import jax
import jax.numpy as jnp
from jax import lax
from jax.experimental import pallas as pl
from jax.experimental.pallas import tpu as pltpu
from jax.sharding import Mesh
from jax.sharding import PartitionSpec as P

ORDER = 6
BUILD = ("build_0", "build_1", "build_2")
BUILD_PROP = ("build_0", "build_1", "build_2", "prop")


def spread(value, axis):
    count = lax.axis_size(axis)
    copies = jnp.broadcast_to(value[None], (count, *value.shape))
    return lax.all_to_all(copies, axis, split_axis=0, concat_axis=0, tiled=True)


def summed_over(value, axis):
    return jnp.sum(spread(value, axis), axis=0)


def tiles_kernel(rows, picks_ref, coeffs_ref, vectors_ref, out_ref):
    count, vectors = coeffs_ref.shape
    deep = vectors_ref.shape[0]
    high = picks_ref.shape[0]
    group = lax.broadcasted_iota(jnp.int32, (vectors, deep), 1) // rows
    widen = (group == lax.broadcasted_iota(jnp.int32, (vectors, deep), 0)).astype(jnp.bfloat16)
    wide = jnp.dot(coeffs_ref[...], widen, preferred_element_type=jnp.float32).astype(jnp.bfloat16)
    walker = lax.broadcasted_iota(jnp.int32, (high, count), 1)
    chosen = (walker == picks_ref[...]).astype(jnp.bfloat16)
    spread_out = jnp.dot(chosen, wide, preferred_element_type=jnp.float32)
    row = lax.broadcasted_iota(jnp.int32, (high, deep), 0) % rows
    column = lax.broadcasted_iota(jnp.int32, (high, deep), 1) % rows
    left = jnp.where(row == column, spread_out, 0.0).astype(jnp.bfloat16)
    out_ref[...] = jnp.dot(left, vectors_ref[...], preferred_element_type=jnp.float32).astype(
        out_ref.dtype
    )


def potential_tiles(picks, coeffs, cholesky):
    vectors, rows, orbitals = cholesky.shape
    count = coeffs.shape[0]
    flat = cholesky.reshape(vectors * rows, orbitals)
    block = 256
    tiles = pl.pallas_call(
        functools.partial(tiles_kernel, rows),
        grid=(count * rows // block,),
        in_specs=[
            pl.BlockSpec((block, 1), lambda i: (i, 0)),
            pl.BlockSpec((count, vectors), lambda i: (0, 0)),
            pl.BlockSpec((vectors * rows, orbitals), lambda i: (0, 0)),
        ],
        out_specs=pl.BlockSpec((block, orbitals), lambda i: (i, 0)),
        out_shape=jax.ShapeDtypeStruct((count * rows, orbitals), jnp.bfloat16),
        name="tiles",
    )(picks, coeffs, flat)
    return tiles.reshape(count, rows, orbitals)


def series_kernel(potential_ref, state_ref, out_ref, total_ref, term_ref):
    orbitals = potential_ref.shape[0]
    block = 256
    for degree in range(1, ORDER + 1):
        source = state_ref if degree == 1 else term_ref.at[(degree - 1) % 2]
        held = source[...]
        for at in range(0, orbitals, block):
            here = pl.ds(at, block)
            product = jnp.dot(potential_ref[here, :], held, preferred_element_type=jnp.float32)
            product = product / degree
            before = state_ref[here, :].astype(jnp.float32) if degree == 1 else total_ref[here, :]
            if degree == ORDER:
                out_ref[here, :] = (before + product).astype(out_ref.dtype)
            else:
                total_ref[here, :] = before + product
                term_ref[degree % 2, here, :] = product.astype(jnp.bfloat16)


def series(potential, state):
    orbitals, electrons = state.shape
    whole = pl.BlockSpec(memory_space=pltpu.VMEM)
    return pl.pallas_call(
        series_kernel,
        in_specs=[whole, whole],
        out_specs=whole,
        out_shape=jax.ShapeDtypeStruct((orbitals, electrons), jnp.bfloat16),
        scratch_shapes=[
            pltpu.VMEM((orbitals, electrons), jnp.float32),
            pltpu.VMEM((2, orbitals, electrons), jnp.bfloat16),
        ],
        name="series",
    )(potential, state)


def of_group(values, member, build_count, prop_count):
    split = values.reshape(build_count, prop_count, *values.shape[1:])
    return lax.dynamic_index_in_dim(split, member, 1, False)


def shards(cholesky, half_vectors, walkers, inverse_intersection, fields, weights, sources):
    build_count = lax.axis_size(BUILD)
    prop_count = lax.axis_size("prop")
    builder = lax.axis_index(BUILD)
    member = lax.axis_index("prop")
    orbitals = walkers.shape[1]
    electrons = walkers.shape[2]
    rows = orbitals // build_count
    own_state = walkers[0]
    theta = jnp.dot(
        own_state, inverse_intersection[0], preferred_element_type=jnp.float32
    ).astype(jnp.bfloat16)
    send = functools.partial(
        lax.all_to_all, axis_name=BUILD, split_axis=0, concat_axis=0, tiled=True
    )
    got_theta = send(theta.reshape(build_count, rows, electrons))
    got_state = send(own_state.reshape(build_count, rows, electrons))
    group_fields = of_group(fields, member, build_count, prop_count)
    group_weights = of_group(weights, member, build_count, prop_count)
    group_sources = of_group(sources, member, build_count, prop_count) // prop_count
    partial_bias = jnp.einsum(
        "wri,gri->wg", got_theta, half_vectors, preferred_element_type=jnp.float32
    )
    force_bias = summed_over(partial_bias, ("build_1", "build_2"))
    force_bias = summed_over(force_bias, "build_0")
    coeffs = (group_fields - force_bias).astype(jnp.bfloat16)
    picks = jnp.repeat(group_sources, rows)[:, None]
    tiles = potential_tiles(picks, coeffs, cholesky)
    starts = got_state.at[group_sources].get(mode="promise_in_bounds")
    begin_state = send(starts).reshape(orbitals, electrons)
    potential = send(tiles).reshape(orbitals, orbitals)
    exponent = jnp.sum(force_bias * (group_fields - 0.5 * force_bias), axis=-1)
    grown = group_weights * jnp.exp(exponent)
    overall = summed_over(jnp.sum(grown)[None], "prop")
    own_source = lax.dynamic_index_in_dim(group_sources, builder, 0, False)
    kept = lax.dynamic_index_in_dim(grown, own_source, 0, False)
    new_weight = kept * (build_count * prop_count) / overall
    stepped = series(potential, begin_state)
    return (stepped[None], new_weight.reshape(1))


def solution(mesh):
    torus = Mesh(
        mesh.devices.reshape(8, 8, 2, mesh.shape["prop"]), ("build_0", "build_1", "build_2", "prop")
    )
    return jax.shard_map(
        shards,
        mesh=torus,
        in_specs=(
            P(None, BUILD, None),
            P(None, BUILD, None),
            P(BUILD_PROP, None, None),
            P(BUILD_PROP, None, None),
            P(),
            P(),
            P(),
        ),
        out_specs=(P(BUILD_PROP, None, None), P(BUILD_PROP)),
        check_vma=False,
    )
```

time: 451 us -> 413 us (0.916)
  the two profiles are of different devices: /device:TPU:28 before, /device:TPU:152 now
where the time goes in v1:
time: 413 us; the launch traced here: 412 us
  waiting for transfers between devices  268 us (65%)
  blocking collectives  59.3 us (14%)
  starting transfers between devices  38 us (9%)
  Pallas kernels  30.6 us (7%)
  local copies, waits for them, and re-layouts  7.11 us (2%)
  between operations  5.22 us (1%)
    all_to_all x1, waiting for transfers between devices, shards(): potential = send(tiles).reshape(orbitals, orbitals)  245 us
    all_to_all x1, blocking collectives, shards(): got_theta = send(theta.reshape(build_count, rows, electrons))  32.6 us
    all_to_all x2, blocking collectives, spread(): return lax.all_to_all(copies, axis, split_axis=0, concat_axis=0, tiled=True)  26.7 us
    pallas_call x1, Pallas kernels, series(): pl.pallas_call(series_kernel, in_specs=[whole, whole], out_specs=whole, o...  17.5 us
    all_to_all x1, waiting for transfers between devices, shards(): got_state = send(own_state.reshape(build_count, rows, electrons))  17.3 us
    all_to_all x1, starting transfers between devices, shards(): potential = send(tiles).reshape(orbitals, orbitals)  13.7 us
    pallas_call x1, Pallas kernels, potential_tiles(): pl.pallas_call(functools.partial(tiles_kernel, rows), grid=(count * rows...  13.1 us
    all_to_all x1, starting transfers between devices, shards(): begin_state = send(starts).reshape(orbitals, electrons)  11 us
  transfers between devices with their start and end apart: 4, of which 4 were waited for; matrix products, arithmetic and copies ran while one was open for 2% of the time, Pallas kernels for 3%

profile of v1, /device:TPU:152, one launch (start us, length us, event | category | flops | bytes accessed | tf_op | source)
XLA Modules:
  0.0 411.9 jit_solution(2066486215343470232)
XLA Ops:
  0.7 1.4 convolution_convert_fusion
  2.0 32.6 %all_to_all.36 = bf16[128,16,128]{2,1,0:T(8,128)(2,1)S(1)} all-to-all(bf16[128,16,128]{2,1,0:T(8,128)(2,1)S(1)} %bitcast.24), channel_id=1, replica_groups=mesh['build_0'=8,'build_1'=8,'build_2'=2,'prop'=4] {'build_0','build_1',..., dimensions={0} | all-to-all | bytes 1048576 | tf_op jit(solution)/shard_map/all_to_all | solution.py:118
  35.0 17.3 %all_to_all.37 = f32[16,128,48]{1,2,0:T(8,128)S(1)} all-to-all(f32[16,128,48]{1,2,0:T(8,128)S(1)} %broadcast_in_dim.11), channel_id=1, replica_groups=mesh['build_0'=8,'build_1'=8,'build_2'=2,'prop'=4] {'build_1','build_2'}, dimensions={0} | all-to-all | bytes 786432 | tf_op jit(solution)/shard_map/all_to_all | solution.py:19
  52.3 8.5 %all-to-all-start.4 = ((bf16[128,16,128]{2,1,0:T(8,128)(2,1)}), bf16[128,16,128]{2,1,0:T(8,128)(2,1)S(1)}, u32[]{:S(2)}, u32[]{:S(2)}) async-start(bf16[128,16,128]{2,1,0:T(8,128)(2,1)} %bitcast.23), calls=%async_computation.4 | async-start | bytes 1048576 | tf_op jit(solution)/shard_map/all_to_all | solution.py:119
  60.8 17.3 %all-to-all-done.4 = bf16[128,16,128]{2,1,0:T(8,128)(2,1)S(1)} async-done(((bf16[128,16,128]{2,1,0:T(8,128)(2,1)}), bf16[128,16,128]{2,1,0:T(8,128)(2,1)S(1)}, u32[]{:S(2)}, u32[]{:S(2)}) %all-to-all-start.4) | async-done | bytes 524320 | tf_op jit(solution)/shard_map/all_to_all | solution.py:119
  78.1 0.7 broadcast_in_dim.12
  78.8 4.8 %all-to-all-start.2 = ((f32[8,128,48]{1,2,0:T(8,128)}), f32[8,128,48]{1,2,0:T(8,128)S(1)}, u32[]{:S(2)}, u32[]{:S(2)}) async-start(f32[8,128,48]{1,2,0:T(8,128)} %broadcast_in_dim.12), calls=%async_computation.2 | async-start | bytes 393216 | tf_op jit(solution)/shard_map/all_to_all | solution.py:19
  83.6 0.8 reshape.39
  84.6 1.5 gather_fusion
  86.1 4.9 %all-to-all-done.2 = f32[8,128,48]{1,2,0:T(8,128)S(1)} async-done(((f32[8,128,48]{1,2,0:T(8,128)}), f32[8,128,48]{1,2,0:T(8,128)S(1)}, u32[]{:S(2)}, u32[]{:S(2)}) %all-to-all-start.2) | async-done | bytes 196640 | tf_op jit(solution)/shard_map/all_to_all | solution.py:19
  91.0 11.0 %all-to-all-start.5 = ((bf16[128,16,128]{2,1,0:T(8,128)(2,1)}), bf16[128,16,128]{2,1,0:T(8,128)(2,1)S(1)}, u32[]{:S(2)}, u32[]{:S(2)}) async-start(bf16[128,16,128]{2,1,0:T(8,128)(2,1)} %gather_fusion), calls=%async_computation.5 | async-start | bytes 1048576 | tf_op jit(solution)/shard_map/all_to_all | solution.py:132
  102.4 1.7 broadcast_in_dim_reshape.4.picks_ref
  104.4 0.6 multiply_reduce_fusion
  105.1 13.1 %tiles.1 = bf16[2048,2048]{1,0:T(8,128)(2,1)} custom-call(s32[2048,1]{1,0:T(8,128)} %broadcast_in_dim_reshape.4.picks_ref, bf16[128,48]{1,0:T(8,128)(2,1)} %get-tuple-element.7.coeffs_ref, bf16[768,2048]{1,0:T(8,128)(2,1)} %bitcast.21), custom_call_target="tpu_custom_call" | custom-call | tf_op jit(solution)/shard_map/tiles/pallas_call | solution.py:49
  118.1 0.6 fusion.7
  118.7 0.7 all-to-all-done.5
  119.4 0.6 broadcast_in_dim.28
  120.1 9.4 %all_to_all.38 = f32[4,1,1]{2,1,0:T(1,128)S(1)} all-to-all(f32[4,1,1]{2,1,0:T(1,128)S(1)} %broadcast_in_dim.28), channel_id=1, replica_groups=mesh['build_0'=8,'build_1'=8,'build_2'=2,'prop'=4] {'prop'}, dimensions={0} | all-to-all | bytes 32 | tf_op jit(solution)/shard_map/all_to_all | solution.py:19
  129.4 13.7 %all-to-all-start.3 = ((bf16[128,16,2048]{2,1,0:T(8,128)(2,1)}), bf16[128,16,2048]{2,1,0:T(8,128)(2,1)}, u32[]{:S(2)}, u32[]{:S(2)}) async-start(bf16[128,16,2048]{2,1,0:T(8,128)(2,1)} %bitcast.20), calls=%async_computation.3 | async-start | bytes 16777216 | tf_op jit(solution)/shard_map/all_to_all | solution.py:133
  143.1 0.6 dynamic_slice.23
  145.7 0.6 dynamic_slice.24
  146.9 0.6 reduce_sum.49
  148.2 245.0 %all-to-all-done.3 = bf16[128,16,2048]{2,1,0:T(8,128)(2,1)} async-done(((bf16[128,16,2048]{2,1,0:T(8,128)(2,1)}), bf16[128,16,2048]{2,1,0:T(8,128)(2,1)}, u32[]{:S(2)}, u32[]{:S(2)}) %all-to-all-start.3) | async-done | bytes 8388640 | tf_op jit(solution)/shard_map/all_to_all | solution.py:133
  393.2 17.5 %series.1 = bf16[2048,128]{1,0:T(8,128)(2,1)} custom-call(bf16[2048,2048]{1,0:T(8,128)(2,1)} %bitcast.8.potential_ref, bf16[2048,128]{1,0:T(8,128)(2,1)} %bitcast.22), custom_call_target="tpu_custom_call" | custom-call | tf_op jit(solution)/shard_map/series/pallas_call | solution.py:85
  (21 shorter events, 1.2 us)
Async XLA Ops:
  0.6 34.0 %copy-start = (bf16[48,16,128]{2,1,0:T(8,128)(2,1)S(1)}, bf16[48,16,128]{2,1,0:T(8,128)(2,1)}, u32[]{:S(2)}) copy-start(bf16[48,16,128]{2,1,0:T(8,128)(2,1)} %param.8) | copy-start | bytes 589828
  0.6 101.4 %copy-start.2 = (f32[512,48]{0,1:T(8,128)S(1)}, f32[512,48]{0,1:T(8,128)}, u32[]{:S(2)}) copy-start(f32[512,48]{0,1:T(8,128)} %param.11) | copy-start | bytes 294916
  0.7 101.5 %copy-start.3 = (f32[512]{0:T(512)S(1)}, f32[512]{0:T(512)}, u32[]{:S(2)}) copy-start(f32[512]{0:T(512)} %param.12) | copy-start | bytes 6148
  52.3 25.8 %all-to-all-start.4 = ((bf16[128,16,128]{2,1,0:T(8,128)(2,1)}), bf16[128,16,128]{2,1,0:T(8,128)(2,1)S(1)}, u32[]{:S(2)}, u32[]{:S(2)}) async-start(bf16[128,16,128]{2,1,0:T(8,128)(2,1)} %bitcast.23), calls=%async_computation.4 | async-start | bytes 1048576 | tf_op jit(solution)/shard_map/all_to_all | solution.py:119
  78.8 12.2 %all-to-all-start.2 = ((f32[8,128,48]{1,2,0:T(8,128)}), f32[8,128,48]{1,2,0:T(8,128)S(1)}, u32[]{:S(2)}, u32[]{:S(2)}) async-start(f32[8,128,48]{1,2,0:T(8,128)} %broadcast_in_dim.12), calls=%async_computation.2 | async-start | bytes 393216 | tf_op jit(solution)/shard_map/all_to_all | solution.py:19
  91.0 28.4 %all-to-all-start.5 = ((bf16[128,16,128]{2,1,0:T(8,128)(2,1)}), bf16[128,16,128]{2,1,0:T(8,128)(2,1)S(1)}, u32[]{:S(2)}, u32[]{:S(2)}) async-start(bf16[128,16,128]{2,1,0:T(8,128)(2,1)} %gather_fusion), calls=%async_computation.5 | async-start | bytes 1048576 | tf_op jit(solution)/shard_map/all_to_all | solution.py:132
  119.4 10.0 %copy-start.1 = (bf16[128,16,128]{2,1,0:T(8,128)(2,1)}, bf16[128,16,128]{2,1,0:T(8,128)(2,1)S(1)}, u32[]{:S(2)}) copy-start(bf16[128,16,128]{2,1,0:T(8,128)(2,1)S(1)} %all-to-all-done.5) | copy-start | bytes 1572868
  129.4 263.8 %all-to-all-start.3 = ((bf16[128,16,2048]{2,1,0:T(8,128)(2,1)}), bf16[128,16,2048]{2,1,0:T(8,128)(2,1)}, u32[]{:S(2)}, u32[]{:S(2)}) async-start(bf16[128,16,2048]{2,1,0:T(8,128)(2,1)} %bitcast.20), calls=%async_computation.3 | async-start | bytes 16777216 | tf_op jit(solution)/shard_map/all_to_all | solution.py:133

commit v2 on v1

--- a/solution.py
+++ b/solution.py
@@ -19,45 +19,77 @@
     return lax.all_to_all(copies, axis, split_axis=0, concat_axis=0, tiled=True)
 
 
-def summed_over(value, axis):
-    return jnp.sum(spread(value, axis), axis=0)
+def theta_kernel(state_ref, inverse_ref, out_ref):
+    electrons = state_ref.shape[1]
+    state = state_ref[...]
+    out_ref[:, :electrons] = jnp.dot(
+        state, inverse_ref[...], preferred_element_type=jnp.float32
+    ).astype(out_ref.dtype)
+    out_ref[:, electrons:] = state
 
 
-def tiles_kernel(rows, picks_ref, coeffs_ref, vectors_ref, out_ref):
+def theta_and_state(state, inverse):
+    orbitals, electrons = state.shape
+    block = 512
+    return pl.pallas_call(
+        theta_kernel,
+        grid=(orbitals // block,),
+        in_specs=[
+            pl.BlockSpec((block, electrons), lambda i: (i, 0)),
+            pl.BlockSpec((electrons, electrons), lambda i: (0, 0)),
+        ],
+        out_specs=pl.BlockSpec((block, 2 * electrons), lambda i: (i, 0)),
+        out_shape=jax.ShapeDtypeStruct((orbitals, 2 * electrons), state.dtype),
+        name="theta",
+    )(state, inverse)
+
+
+def tiles_kernel(rows, chosen_ref, coeffs_ref, vectors_ref, out_ref, wide_ref):
     count, vectors = coeffs_ref.shape
     deep = vectors_ref.shape[0]
-    high = picks_ref.shape[0]
-    group = lax.broadcasted_iota(jnp.int32, (vectors, deep), 1) // rows
-    widen = (group == lax.broadcasted_iota(jnp.int32, (vectors, deep), 0)).astype(jnp.bfloat16)
-    wide = jnp.dot(coeffs_ref[...], widen, preferred_element_type=jnp.float32).astype(jnp.bfloat16)
-    walker = lax.broadcasted_iota(jnp.int32, (high, count), 1)
-    chosen = (walker == picks_ref[...]).astype(jnp.bfloat16)
-    spread_out = jnp.dot(chosen, wide, preferred_element_type=jnp.float32)
-    row = lax.broadcasted_iota(jnp.int32, (high, deep), 0) % rows
-    column = lax.broadcasted_iota(jnp.int32, (high, deep), 1) % rows
-    left = jnp.where(row == column, spread_out, 0.0).astype(jnp.bfloat16)
+    block = out_ref.shape[0]
+    few = block // rows
+    shift = rows.bit_length() - 1
+    step = pl.program_id(0)
+
+    @pl.when(step == 0)
+    def _():
+        group = lax.broadcasted_iota(jnp.int32, (vectors, deep), 1) >> shift
+        vector = lax.broadcasted_iota(jnp.int32, (vectors, deep), 0)
+        widen = (group == vector).astype(jnp.bfloat16)
+        picked = jnp.dot(chosen_ref[...], coeffs_ref[...], preferred_element_type=jnp.float32)
+        wide_ref[...] = jnp.dot(
+            picked.astype(jnp.bfloat16), widen, preferred_element_type=jnp.float32
+        ).astype(jnp.bfloat16)
+
+    owner = lax.broadcasted_iota(jnp.int32, (block, few), 0) >> shift
+    repeat = (owner == lax.broadcasted_iota(jnp.int32, (block, few), 1)).astype(jnp.bfloat16)
+    row = lax.broadcasted_iota(jnp.int32, (block, deep), 0) & (rows - 1)
+    column = lax.broadcasted_iota(jnp.int32, (block, deep), 1) & (rows - 1)
+    here = wide_ref[pl.ds(pl.multiple_of(step * few, few), few), :]
+    left = jnp.dot(repeat, here, preferred_element_type=jnp.float32)
+    left = jnp.where(row == column, left, 0.0).astype(jnp.bfloat16)
     out_ref[...] = jnp.dot(left, vectors_ref[...], preferred_element_type=jnp.float32).astype(
         out_ref.dtype
     )
 
 
-def potential_tiles(picks, coeffs, cholesky):
+def potential_tiles(chosen, coeffs, cholesky):
     vectors, rows, orbitals = cholesky.shape
     count = coeffs.shape[0]
     flat = cholesky.reshape(vectors * rows, orbitals)
     block = 256
+    whole = pl.BlockSpec(memory_space=pltpu.VMEM)
     tiles = pl.pallas_call(
         functools.partial(tiles_kernel, rows),
         grid=(count * rows // block,),
-        in_specs=[
-            pl.BlockSpec((block, 1), lambda i: (i, 0)),
-            pl.BlockSpec((count, vectors), lambda i: (0, 0)),
-            pl.BlockSpec((vectors * rows, orbitals), lambda i: (0, 0)),
-        ],
+        in_specs=[whole, whole, whole],
         out_specs=pl.BlockSpec((block, orbitals), lambda i: (i, 0)),
-        out_shape=jax.ShapeDtypeStruct((count * rows, orbitals), jnp.bfloat16),
+        out_shape=pltpu.HBM((count * rows, orbitals), jnp.bfloat16),
+        scratch_shapes=[pltpu.VMEM((count, vectors * rows), jnp.bfloat16)],
+        compiler_params=pltpu.CompilerParams(vmem_limit_bytes=16 << 20),
         name="tiles",
-    )(picks, coeffs, flat)
+    )(chosen, coeffs, flat)
     return tiles.reshape(count, rows, orbitals)
 
 
@@ -91,8 +123,9 @@
             pltpu.VMEM((orbitals, electrons), jnp.float32),
             pltpu.VMEM((2, orbitals, electrons), jnp.bfloat16),
         ],
+        compiler_params=pltpu.CompilerParams(vmem_limit_bytes=16 << 20),
         name="series",
-    )(potential, state)
+    )(pltpu.with_memory_space_constraint(potential, pltpu.VMEM), state)
 
 
 def of_group(values, member, build_count, prop_count):
@@ -108,35 +141,35 @@
     orbitals = walkers.shape[1]
     electrons = walkers.shape[2]
     rows = orbitals // build_count
-    own_state = walkers[0]
-    theta = jnp.dot(
-        own_state, inverse_intersection[0], preferred_element_type=jnp.float32
-    ).astype(jnp.bfloat16)
     send = functools.partial(
         lax.all_to_all, axis_name=BUILD, split_axis=0, concat_axis=0, tiled=True
     )
-    got_theta = send(theta.reshape(build_count, rows, electrons))
-    got_state = send(own_state.reshape(build_count, rows, electrons))
+    outgoing = theta_and_state(walkers[0], inverse_intersection[0])
+    got = send(outgoing.reshape(build_count, rows, 2 * electrons))
+    got_theta, got_state = got[:, :, :electrons], got[:, :, electrons:]
     group_fields = of_group(fields, member, build_count, prop_count)
     group_weights = of_group(weights, member, build_count, prop_count)
     group_sources = of_group(sources, member, build_count, prop_count) // prop_count
     partial_bias = jnp.einsum(
-        "wri,gri->wg", got_theta, half_vectors, preferred_element_type=jnp.float32
+        "wri,gri->gw", got_theta, half_vectors, preferred_element_type=jnp.float32
     )
-    force_bias = summed_over(partial_bias, ("build_1", "build_2"))
-    force_bias = summed_over(force_bias, "build_0")
+    starts = got_state.at[group_sources].get(mode="promise_in_bounds")
+    starts, partial_bias = lax.optimization_barrier((starts, partial_bias))
+    begin_state = send(starts).reshape(orbitals, electrons)
+    line_bias = jnp.sum(lax.all_gather(partial_bias, ("build_1", "build_2")), axis=0)
+    begin_state, line_bias = lax.optimization_barrier((begin_state, line_bias))
+    force_bias = jnp.sum(spread(line_bias, "build_0"), axis=0).T
     coeffs = (group_fields - force_bias).astype(jnp.bfloat16)
-    picks = jnp.repeat(group_sources, rows)[:, None]
-    tiles = potential_tiles(picks, coeffs, cholesky)
-    starts = got_state.at[group_sources].get(mode="promise_in_bounds")
-    begin_state = send(starts).reshape(orbitals, electrons)
-    potential = send(tiles).reshape(orbitals, orbitals)
+    chosen = group_sources[:, None] == jnp.arange(build_count, dtype=jnp.int32)[None]
+    tiles = potential_tiles(chosen.astype(jnp.bfloat16), coeffs, cholesky)
     exponent = jnp.sum(force_bias * (group_fields - 0.5 * force_bias), axis=-1)
     grown = group_weights * jnp.exp(exponent)
-    overall = summed_over(jnp.sum(grown)[None], "prop")
+    overall = jnp.sum(spread(jnp.sum(grown)[None], "prop"), axis=0)
     own_source = lax.dynamic_index_in_dim(group_sources, builder, 0, False)
     kept = lax.dynamic_index_in_dim(grown, own_source, 0, False)
     new_weight = kept * (build_count * prop_count) / overall
+    tiles, begin_state, new_weight = lax.optimization_barrier((tiles, begin_state, new_weight))
+    potential = send(tiles).reshape(orbitals, orbitals)
     stepped = series(potential, begin_state)
     return (stepped[None], new_weight.reshape(1))
 

time: 413 us -> 361 us (0.87)
  the two profiles are of different devices: /device:TPU:152 before, /device:TPU:43 now
where the time goes in v2:
time: 361 us; the launch traced here: 360 us
  blocking collectives  241 us (67%)
  starting transfers between devices  37.7 us (10%)
  waiting for transfers between devices  32.4 us (9%)
  Pallas kernels  28.9 us (8%)
  local copies, waits for them, and re-layouts  10.8 us (3%)
  between operations  5.22 us (1%)
  other arithmetic  3.7 us (1%)
    all_to_all x1, blocking collectives, shards(): potential = send(tiles).reshape(orbitals, orbitals)  216 us
    all_to_all x1, waiting for transfers between devices, shards(): got = send(outgoing.reshape(build_count, rows, 2 * electrons))  27.3 us
    all_gather x1, blocking collectives, shards(): lax.all_gather(partial_bias, ('build_1', 'build_2'))  24.8 us
    all_to_all x1, starting transfers between devices, shards(): got = send(outgoing.reshape(build_count, rows, 2 * electrons))  17.7 us
    pallas_call x1, Pallas kernels, series(): pl.pallas_call(series_kernel, in_specs=[whole, whole], out_specs=whole, o...  15.1 us
    all_to_all x2, starting transfers between devices, spread(): return lax.all_to_all(copies, axis, split_axis=0, concat_axis=0, tiled=True)  11 us
    pallas_call x1, Pallas kernels, potential_tiles(): pl.pallas_call(functools.partial(tiles_kernel, rows), grid=(count * rows...  10 us
    all_to_all x1, starting transfers between devices, shards(): begin_state = send(starts).reshape(orbitals, electrons)  9.01 us
  transfers between devices with their start and end apart: 4, of which 2 were waited for; matrix products, arithmetic and copies ran while one was open for 2% of the time, Pallas kernels for 3%

profile of v2, /device:TPU:43, one launch (start us, length us, event | category | flops | bytes accessed | tf_op | source)
XLA Modules:
  0.0 360.2 jit_solution(13104722934935785159)
XLA Ops:
  0.7 3.8 %theta.1 = bf16[2048,256]{1,0:T(8,128)(2,1)} custom-call(bf16[2048,128]{1,0:T(8,128)(2,1)} %bitcast.35, bf16[128,128]{1,0:T(8,128)(2,1)} %bitcast.39), custom_call_target="tpu_custom_call" | custom-call | tf_op jit(solution)/shard_map/theta/pallas_call | solution.py:34
  4.4 17.7 %all-to-all-start = ((bf16[128,16,256]{2,1,0:T(8,128)(2,1)}), bf16[128,16,256]{2,1,0:T(8,128)(2,1)}, u32[]{:S(2)}, u32[]{:S(2)}) async-start(bf16[128,16,256]{2,1,0:T(8,128)(2,1)} %bitcast.33), calls=%async_computation | async-start | bytes 2097152 | tf_op jit(solution)/shard_map/all_to_all | solution.py:148
  22.1 0.8 reshape.38
  23.2 27.3 %all-to-all-done = bf16[128,16,256]{2,1,0:T(8,128)(2,1)} async-done(((bf16[128,16,256]{2,1,0:T(8,128)(2,1)}), bf16[128,16,256]{2,1,0:T(8,128)(2,1)}, u32[]{:S(2)}, u32[]{:S(2)}) %all-to-all-start) | async-done | bytes 1048608 | tf_op jit(solution)/shard_map/all_to_all | solution.py:148
  50.6 2.2 fusion.10
  53.0 2.5 gather_fusion
  55.6 9.0 %all-to-all-start.1 = ((bf16[128,16,128]{2,1,0:T(8,128)(2,1)}), bf16[128,16,128]{2,1,0:T(8,128)(2,1)}, u32[]{:S(2)}, u32[]{:S(2)}) async-start(bf16[128,16,128]{2,1,0:T(8,128)(2,1)} %gather_fusion), calls=%async_computation.1 | async-start | bytes 1048576 | tf_op jit(solution)/shard_map/all_to_all | solution.py:158
  64.6 24.8 %all-gather = f32[768,128]{1,0:T(8,128)} all-gather(f32[48,128]{1,0:T(8,128)S(1)} %convolution_bitcast_fusion), channel_id=2, replica_groups=mesh['build_0'=8,'build_1'=8,'build_2'=2,'prop'=4] {'build_1','build_2'}, dimensions={0}, use_global_device_ids=true | all-gather | bytes 417792 | tf_op jit(solution)/shard_map/all_gather | solution.py:159
  89.3 1.0 reduce_sum.45
  90.4 0.7 broadcast_in_dim.6
  91.1 6.8 %all-to-all-start.2 = ((f32[8,48,128]{2,1,0:T(8,128)}), f32[8,48,128]{2,1,0:T(8,128)}, u32[]{:S(2)}, u32[]{:S(2)}) async-start(f32[8,48,128]{2,1,0:T(8,128)} %broadcast_in_dim.6), calls=%async_computation.2 | async-start | bytes 393216 | tf_op jit(solution)/shard_map/all_to_all | solution.py:19
  97.9 0.6 dynamic_slice.23
  99.9 0.8 copy.28
  101.5 1.0 constant_dynamic-slice_fusion
  102.6 5.1 %all-to-all-done.2 = f32[8,48,128]{2,1,0:T(8,128)} async-done(((f32[8,48,128]{2,1,0:T(8,128)}), f32[8,48,128]{2,1,0:T(8,128)}, u32[]{:S(2)}, u32[]{:S(2)}) %all-to-all-start.2) | async-done | bytes 196640 | tf_op jit(solution)/shard_map/all_to_all | solution.py:19
  107.7 0.9 reduce_sum.46
  108.9 0.6 fusion.9
  109.5 1.2 broadcast_in_dim.7
  110.7 4.3 %all-to-all-start.3 = ((f32[4,1,1]{2,1,0:T(1,128)}), f32[4,1,1]{2,1,0:T(1,128)S(1)}, u32[]{:S(2)}, u32[]{:S(2)}) async-start(f32[4,1,1]{2,1,0:T(1,128)} %broadcast_in_dim.7), calls=%async_computation.3 | async-start | bytes 4096 | tf_op jit(solution)/shard_map/all_to_all | solution.py:19
  115.0 0.6 dynamic_slice.24
  116.2 10.0 %tiles.1 = bf16[2048,2048]{1,0:T(8,128)(2,1)} custom-call(bf16[128,128]{1,0:T(8,128)(2,1)S(1)} %fusion.8.chosen_ref, bf16[128,48]{1,0:T(8,128)(2,1)S(1)} %get-tuple-element.23.coeffs_ref, bf16[768,2048]{1,0:T(8,128)(2,1)S(1)} %bitcast.31), custom_call_target="tpu_custom_call" | custom-call | tf_op jit(solution)/shard_map/tiles/pallas_call | solution.py:83
  126.2 0.6 reduce_sum.49
  127.5 216.4 %all_to_all.26 = bf16[128,16,2048]{2,1,0:T(8,128)(2,1)S(1)} all-to-all(bf16[128,16,2048]{2,1,0:T(8,128)(2,1)} %bitcast.32), channel_id=1, replica_groups=mesh['build_0'=8,'build_1'=8,'build_2'=2,'prop'=4] {'build_0','build_1',..., dimensions={0} | all-to-all | bytes 16777216 | tf_op jit(solution)/shard_map/all_to_all | solution.py:172
  344.0 15.1 %series.1 = bf16[2048,128]{1,0:T(8,128)(2,1)} custom-call(bf16[2048,2048]{1,0:T(8,128)(2,1)S(1)} %bitcast.30, bf16[2048,128]{1,0:T(8,128)(2,1)} %bitcast.7.state_ref), custom_call_target="tpu_custom_call" | custom-call | tf_op jit(solution)/shard_map/series/pallas_call | solution.py:117
  (20 shorter events, 1.2 us)
Async XLA Ops:
  0.6 52.1 %copy-start = (bf16[48,16,128]{2,1,0:T(8,128)(2,1)S(1)}, bf16[48,16,128]{2,1,0:T(8,128)(2,1)}, u32[]{:S(2)}) copy-start(bf16[48,16,128]{2,1,0:T(8,128)(2,1)} %param.8) | copy-start | bytes 589828
  0.6 99.1 %copy-start.3 = (f32[512]{0:T(512)S(1)}, f32[512]{0:T(512)}, u32[]{:S(2)}) copy-start(f32[512]{0:T(512)} %param.12) | copy-start | bytes 6148
  0.7 99.2 %copy-start.2 = (f32[512,48]{0,1:T(8,128)S(1)}, f32[512,48]{0,1:T(8,128)}, u32[]{:S(2)}) copy-start(f32[512,48]{0,1:T(8,128)} %param.11) | copy-start | bytes 294916
  0.7 115.5 %copy-start.1 = (bf16[48,16,2048]{2,1,0:T(8,128)(2,1)S(1)}, bf16[48,16,2048]{2,1,0:T(8,128)(2,1)}, u32[]{:S(2)}) copy-start(bf16[48,16,2048]{2,1,0:T(8,128)(2,1)} %param.7) | copy-start | bytes 9437188
  4.4 46.1 %all-to-all-start = ((bf16[128,16,256]{2,1,0:T(8,128)(2,1)}), bf16[128,16,256]{2,1,0:T(8,128)(2,1)}, u32[]{:S(2)}, u32[]{:S(2)}) async-start(bf16[128,16,256]{2,1,0:T(8,128)(2,1)} %bitcast.33), calls=%async_computation | async-start | bytes 2097152 | tf_op jit(solution)/shard_map/all_to_all | solution.py:148
  55.6 34.8 %all-to-all-start.1 = ((bf16[128,16,128]{2,1,0:T(8,128)(2,1)}), bf16[128,16,128]{2,1,0:T(8,128)(2,1)}, u32[]{:S(2)}, u32[]{:S(2)}) async-start(bf16[128,16,128]{2,1,0:T(8,128)(2,1)} %gather_fusion), calls=%async_computation.1 | async-start | bytes 1048576 | tf_op jit(solution)/shard_map/all_to_all | solution.py:158
  91.1 16.6 %all-to-all-start.2 = ((f32[8,48,128]{2,1,0:T(8,128)}), f32[8,48,128]{2,1,0:T(8,128)}, u32[]{:S(2)}, u32[]{:S(2)}) async-start(f32[8,48,128]{2,1,0:T(8,128)} %broadcast_in_dim.6), calls=%async_computation.2 | async-start | bytes 393216 | tf_op jit(solution)/shard_map/all_to_all | solution.py:19
  110.7 15.5 %all-to-all-start.3 = ((f32[4,1,1]{2,1,0:T(1,128)}), f32[4,1,1]{2,1,0:T(1,128)S(1)}, u32[]{:S(2)}, u32[]{:S(2)}) async-start(f32[4,1,1]{2,1,0:T(1,128)} %broadcast_in_dim.7), calls=%async_computation.3 | async-start | bytes 4096 | tf_op jit(solution)/shard_map/all_to_all | solution.py:19

commit v3 on v2

--- a/solution.py
+++ b/solution.py
@@ -11,6 +11,7 @@
 ORDER = 6
 BUILD = ("build_0", "build_1", "build_2")
 BUILD_PROP = ("build_0", "build_1", "build_2", "prop")
+WHOLE = pl.BlockSpec(memory_space=pltpu.VMEM)
 
 
 def spread(value, axis):
@@ -30,38 +31,106 @@
 
 def theta_and_state(state, inverse):
     orbitals, electrons = state.shape
-    block = 512
     return pl.pallas_call(
         theta_kernel,
-        grid=(orbitals // block,),
-        in_specs=[
-            pl.BlockSpec((block, electrons), lambda i: (i, 0)),
-            pl.BlockSpec((electrons, electrons), lambda i: (0, 0)),
-        ],
-        out_specs=pl.BlockSpec((block, 2 * electrons), lambda i: (i, 0)),
+        in_specs=[WHOLE, WHOLE],
+        out_specs=WHOLE,
         out_shape=jax.ShapeDtypeStruct((orbitals, 2 * electrons), state.dtype),
+        compiler_params=pltpu.CompilerParams(vmem_limit_bytes=8 << 20),
         name="theta",
     )(state, inverse)
 
 
-def tiles_kernel(rows, chosen_ref, coeffs_ref, vectors_ref, out_ref, wide_ref):
-    count, vectors = coeffs_ref.shape
+def pick_kernel(prop_count, sources_ref, got_ref, theta_ref, starts_ref):
+    count = got_ref.shape[0]
+    electrons = theta_ref.shape[2]
+    member = lax.axis_index("prop")
+    theta_ref[...] = got_ref[:, :, :electrons]
+
+    def move(w, carry):
+        source = sources_ref[w * prop_count + member] // prop_count
+        starts_ref[w] = got_ref[source, :, electrons:]
+        return carry
+
+    lax.fori_loop(0, count, move, 0, unroll=8)
+
+
+def theta_and_starts(sources, got, prop_count):
+    count, rows, both = got.shape
+    shape = (count, rows, both // 2)
+    return pl.pallas_call(
+        functools.partial(pick_kernel, prop_count),
+        in_specs=[pl.BlockSpec(memory_space=pltpu.SMEM), WHOLE],
+        out_specs=[WHOLE, WHOLE],
+        out_shape=[jax.ShapeDtypeStruct(shape, got.dtype), pltpu.HBM(shape, got.dtype)],
+        compiler_params=pltpu.CompilerParams(vmem_limit_bytes=8 << 20),
+        name="pick",
+    )(sources, got)
+
+
+def merge_kernel(parts_ref, out_ref):
+    total = jnp.sum(parts_ref[...], axis=0)
+    for at in range(out_ref.shape[0]):
+        out_ref[at] = total
+
+
+def summed_copies(parts, copies):
+    return pl.pallas_call(
+        merge_kernel,
+        in_specs=[WHOLE],
+        out_specs=WHOLE,
+        out_shape=pltpu.HBM((copies, *parts.shape[1:]), parts.dtype),
+        compiler_params=pltpu.CompilerParams(vmem_limit_bytes=8 << 20),
+        name="merge",
+    )(parts)
+
+
+def bias_kernel(rows, parts_ref, fields_ref, weights_ref, sources_ref, own_ref, wide_ref, sums_ref, kept_ref):
+    vectors, count = fields_ref.shape
+    deep = wide_ref.shape[1]
+    shift = rows.bit_length() - 1
+    bias = jnp.sum(parts_ref[...], axis=0)
+    fields = fields_ref[...]
+    coeffs = (fields - bias).astype(jnp.bfloat16)
+    exponent = jnp.sum(bias * (fields - 0.5 * bias), axis=0, keepdims=True)
+    grown = weights_ref[...] * jnp.exp(exponent)
+    kept = jnp.sum(grown * own_ref[...], axis=1, keepdims=True)
+    kept_ref[...] = jnp.broadcast_to(kept, kept_ref.shape)
+    total = jnp.sum(grown, axis=1, keepdims=True)
+    sums_ref[...] = jnp.broadcast_to(total[None], sums_ref.shape)
+    walker = lax.broadcasted_iota(jnp.int32, (count, count), 0)
+    chosen = (walker == sources_ref[...]).astype(jnp.bfloat16)
+    picked = jnp.dot(coeffs, chosen, preferred_element_type=jnp.float32).T
+    group = lax.broadcasted_iota(jnp.int32, (vectors, deep), 1) >> shift
+    vector = lax.broadcasted_iota(jnp.int32, (vectors, deep), 0)
+    widen = (group == vector).astype(jnp.bfloat16)
+    wide_ref[...] = jnp.dot(
+        picked.astype(jnp.bfloat16), widen, preferred_element_type=jnp.float32
+    ).astype(jnp.bfloat16)
+
+
+def bias_and_weights(parts, fields, weights, sources, own, rows, prop_count):
+    vectors, count = fields.shape
+    return pl.pallas_call(
+        functools.partial(bias_kernel, rows),
+        in_specs=[WHOLE] * 5,
+        out_specs=[WHOLE] * 3,
+        out_shape=[
+            pltpu.HBM((count, vectors * rows), jnp.bfloat16),
+            pltpu.HBM((prop_count, 1, count), jnp.float32),
+            jax.ShapeDtypeStruct((1, count), jnp.float32),
+        ],
+        compiler_params=pltpu.CompilerParams(vmem_limit_bytes=8 << 20),
+        name="bias",
+    )(parts, fields, weights, sources, own)
+
+
+def tiles_kernel(rows, wide_ref, vectors_ref, out_ref):
     deep = vectors_ref.shape[0]
     block = out_ref.shape[0]
     few = block // rows
     shift = rows.bit_length() - 1
     step = pl.program_id(0)
-
-    @pl.when(step == 0)
-    def _():
-        group = lax.broadcasted_iota(jnp.int32, (vectors, deep), 1) >> shift
-        vector = lax.broadcasted_iota(jnp.int32, (vectors, deep), 0)
-        widen = (group == vector).astype(jnp.bfloat16)
-        picked = jnp.dot(chosen_ref[...], coeffs_ref[...], preferred_element_type=jnp.float32)
-        wide_ref[...] = jnp.dot(
-            picked.astype(jnp.bfloat16), widen, preferred_element_type=jnp.float32
-        ).astype(jnp.bfloat16)
-
     owner = lax.broadcasted_iota(jnp.int32, (block, few), 0) >> shift
     repeat = (owner == lax.broadcasted_iota(jnp.int32, (block, few), 1)).astype(jnp.bfloat16)
     row = lax.broadcasted_iota(jnp.int32, (block, deep), 0) & (rows - 1)
@@ -74,22 +143,20 @@
     )
 
 
-def potential_tiles(chosen, coeffs, cholesky):
+def potential_tiles(wide, cholesky):
     vectors, rows, orbitals = cholesky.shape
-    count = coeffs.shape[0]
+    count = wide.shape[0]
     flat = cholesky.reshape(vectors * rows, orbitals)
     block = 256
-    whole = pl.BlockSpec(memory_space=pltpu.VMEM)
     tiles = pl.pallas_call(
         functools.partial(tiles_kernel, rows),
         grid=(count * rows // block,),
-        in_specs=[whole, whole, whole],
+        in_specs=[WHOLE, WHOLE],
         out_specs=pl.BlockSpec((block, orbitals), lambda i: (i, 0)),
         out_shape=pltpu.HBM((count * rows, orbitals), jnp.bfloat16),
-        scratch_shapes=[pltpu.VMEM((count, vectors * rows), jnp.bfloat16)],
         compiler_params=pltpu.CompilerParams(vmem_limit_bytes=16 << 20),
         name="tiles",
-    )(chosen, coeffs, flat)
+    )(wide, flat)
     return tiles.reshape(count, rows, orbitals)
 
 
@@ -113,11 +180,10 @@
 
 def series(potential, state):
     orbitals, electrons = state.shape
-    whole = pl.BlockSpec(memory_space=pltpu.VMEM)
     return pl.pallas_call(
         series_kernel,
-        in_specs=[whole, whole],
-        out_specs=whole,
+        in_specs=[WHOLE, WHOLE],
+        out_specs=WHOLE,
         out_shape=jax.ShapeDtypeStruct((orbitals, electrons), jnp.bfloat16),
         scratch_shapes=[
             pltpu.VMEM((orbitals, electrons), jnp.float32),
@@ -125,7 +191,7 @@
         ],
         compiler_params=pltpu.CompilerParams(vmem_limit_bytes=16 << 20),
         name="series",
-    )(pltpu.with_memory_space_constraint(potential, pltpu.VMEM), state)
+    )(potential, state)
 
 
 def of_group(values, member, build_count, prop_count):
@@ -146,32 +212,35 @@
     )
     outgoing = theta_and_state(walkers[0], inverse_intersection[0])
     got = send(outgoing.reshape(build_count, rows, 2 * electrons))
-    got_theta, got_state = got[:, :, :electrons], got[:, :, electrons:]
-    group_fields = of_group(fields, member, build_count, prop_count)
-    group_weights = of_group(weights, member, build_count, prop_count)
-    group_sources = of_group(sources, member, build_count, prop_count) // prop_count
+    got_theta, starts = theta_and_starts(sources, got, prop_count)
     partial_bias = jnp.einsum(
         "wri,gri->gw", got_theta, half_vectors, preferred_element_type=jnp.float32
     )
-    starts = got_state.at[group_sources].get(mode="promise_in_bounds")
     starts, partial_bias = lax.optimization_barrier((starts, partial_bias))
     begin_state = send(starts).reshape(orbitals, electrons)
-    line_bias = jnp.sum(lax.all_gather(partial_bias, ("build_1", "build_2")), axis=0)
-    begin_state, line_bias = lax.optimization_barrier((begin_state, line_bias))
-    force_bias = jnp.sum(spread(line_bias, "build_0"), axis=0).T
-    coeffs = (group_fields - force_bias).astype(jnp.bfloat16)
-    chosen = group_sources[:, None] == jnp.arange(build_count, dtype=jnp.int32)[None]
-    tiles = potential_tiles(chosen.astype(jnp.bfloat16), coeffs, cholesky)
-    exponent = jnp.sum(force_bias * (group_fields - 0.5 * force_bias), axis=-1)
-    grown = group_weights * jnp.exp(exponent)
-    overall = jnp.sum(spread(jnp.sum(grown)[None], "prop"), axis=0)
+    line_parts = lax.all_gather(partial_bias, ("build_1", "build_2"))
+    begin_state, line_parts, fields, weights, sources = lax.optimization_barrier(
+        (begin_state, line_parts, fields, weights, sources)
+    )
+    line_bias = summed_copies(line_parts, lax.axis_size("build_0"))
+    parts = lax.all_to_all(line_bias, "build_0", split_axis=0, concat_axis=0, tiled=True)
+    group_fields = of_group(fields, member, build_count, prop_count).T
+    group_weights = of_group(weights, member, build_count, prop_count)[None]
+    group_sources = of_group(sources, member, build_count, prop_count) // prop_count
     own_source = lax.dynamic_index_in_dim(group_sources, builder, 0, False)
-    kept = lax.dynamic_index_in_dim(grown, own_source, 0, False)
-    new_weight = kept * (build_count * prop_count) / overall
+    own = (jnp.arange(build_count, dtype=jnp.int32) == own_source).astype(jnp.float32)
+    wide, sums, kept = bias_and_weights(
+        parts, group_fields, group_weights, group_sources[None], own[None], rows, prop_count
+    )
+    sums = lax.all_to_all(sums, "prop", split_axis=0, concat_axis=0, tiled=True)
+    tiles = potential_tiles(wide, cholesky)
+    overall = jnp.sum(sums[:, 0, :1], axis=0)
+    new_weight = kept[0, :1] * (build_count * prop_count) / overall
     tiles, begin_state, new_weight = lax.optimization_barrier((tiles, begin_state, new_weight))
     potential = send(tiles).reshape(orbitals, orbitals)
+    potential = pltpu.with_memory_space_constraint(potential, pltpu.VMEM)
     stepped = series(potential, begin_state)
-    return (stepped[None], new_weight.reshape(1))
+    return (stepped[None], new_weight)
 
 
 def solution(mesh):

time: 361 us -> 360 us (level)
  blocking collectives: 241 us -> 291 us
  waiting for transfers between devices: 32.4 us -> 0.01 us
  starting transfers between devices: 37.7 us -> 20 us
  local copies, waits for them, and re-layouts: 10.8 us -> 14.9 us
    all_to_all x0 -> x1, blocking collectives: none -> 45.8 us  [shards(): got = send(outgoing.reshape(build_count, rows, 2 * electrons))]
    all_to_all x3 -> x2, waiting for transfers between devices: 32.4 us -> 0.01 us  [the longest x1 0.01 us: shards(): lax.all_to_all(line_bias, 'build_0', split_axis=0, concat_axis=0, tiled=T...]
    all_to_all x3 -> x2, starting transfers between devices: 28.7 us -> 11 us  [the longest x1 6.76 us: shards(): lax.all_to_all(line_bias, 'build_0', split_axis=0, concat_axis=0, tiled=T...]
    unnamed x9 -> x18, local copies, waits for them, and re-layouts: 0.86 us -> 5.29 us
    all_to_all x1, blocking collectives: 216 us -> 221 us  [shards(): potential = send(tiles).reshape(orbitals, orbitals)]
    dynamic_slice x2 -> x4, local copies, waits for them, and re-layouts: 1.19 us -> 5.18 us  [of_group(): return lax.dynamic_index_in_dim(split, member, 1, False)]
    pallas_call x2 -> x5, Pallas kernels: 18.9 us -> 19.4 us  [the longest x1 15.1 us: series(): pl.pallas_call(series_kernel, in_specs=[WHOLE, WHOLE], out_specs=WHOLE, o...]
  transfers between devices with their start and end apart: 4 -> 3, of which waited for: 2 -> 0; matrix products, arithmetic and copies ran while one was open for 2% -> 3% of each run, Pallas kernels for 3% -> 3%
where the time goes in v3:
time: 360 us; the launch traced here: 359 us
  blocking collectives  291 us (81%)
  Pallas kernels  29.1 us (8%)
  starting transfers between devices  20 us (6%)
  local copies, waits for them, and re-layouts  14.9 us (4%)
    all_to_all x1, blocking collectives, shards(): potential = send(tiles).reshape(orbitals, orbitals)  221 us
    all_to_all x1, blocking collectives, shards(): got = send(outgoing.reshape(build_count, rows, 2 * electrons))  45.8 us
    all_gather x1, blocking collectives, shards(): line_parts = lax.all_gather(partial_bias, ('build_1', 'build_2'))  24.7 us
    pallas_call x1, Pallas kernels, series(): pl.pallas_call(series_kernel, in_specs=[WHOLE, WHOLE], out_specs=WHOLE, o...  15.1 us
    pallas_call x1, Pallas kernels, potential_tiles(): pl.pallas_call(functools.partial(tiles_kernel, rows), grid=(count * rows...  9.67 us
    all_to_all x1, starting transfers between devices, shards(): begin_state = send(starts).reshape(orbitals, electrons)  9.02 us
  transfers between devices with their start and end apart: 3, of which 0 were waited for; matrix products, arithmetic and copies ran while one was open for 3% of the time, Pallas kernels for 3%

profile of v3, /device:TPU:43, one launch (start us, length us, event | category | flops | bytes accessed | tf_op | source)
XLA Modules:
  0.0 359.4 jit_solution(15213447802224134318)
XLA Ops:
  0.7 1.2 copy-done.3
  1.9 0.8 copy-done.6
  2.9 45.8 %all_to_all.25.got_ref = bf16[128,16,256]{2,1,0:T(8,128)(2,1)S(1)} all-to-all(bf16[128,16,256]{2,1,0:T(8,128)(2,1)S(1)} %bitcast.31), channel_id=1, replica_groups=mesh['build_0'=8,'build_1'=8,'build_2'=2,'prop'=4] {'build_0','build_1',..., dimensions={0} | all-to-all | bytes 2097152 | tf_op jit(solution)/shard_map/all_to_all | solution.py:214
  48.7 0.7 copy-done.7
  49.4 2.2 pick.1
  52.0 9.0 %all-to-all-start.1 = ((bf16[128,16,128]{2,1,0:T(8,128)(2,1)}), bf16[128,16,128]{2,1,0:T(8,128)(2,1)}, u32[]{:S(2)}, u32[]{:S(2)}) async-start(bf16[128,16,128]{2,1,0:T(8,128)(2,1)} %get-tuple-element.19), calls=%async_computation.1 | async-start | bytes 1048576 | tf_op jit(solution)/shard_map/all_to_all | solution.py:220
  61.0 24.7 %all-gather = f32[768,128]{1,0:T(8,128)} all-gather(f32[48,128]{1,0:T(8,128)S(1)} %convolution_bitcast_fusion), channel_id=2, replica_groups=mesh['build_0'=8,'build_1'=8,'build_2'=2,'prop'=4] {'build_1','build_2'}, dimensions={0}, use_global_device_ids=true | all-gather | bytes 417792 | tf_op jit(solution)/shard_map/all_gather | solution.py:221
  85.8 1.0 copy-done.2
  86.8 0.7 merge.1
  87.5 6.8 %all-to-all-start.2 = ((f32[8,48,128]{2,1,0:T(8,128)}), f32[8,48,128]{2,1,0:T(8,128)S(1)}, u32[]{:S(2)}, u32[]{:S(2)}) async-start(f32[8,48,128]{2,1,0:T(8,128)} %merge.1), calls=%async_computation.2 | async-start | bytes 393216 | tf_op jit(solution)/shard_map/all_to_all | solution.py:226
  94.2 1.4 reshape.116
  95.6 1.0 dynamic-slice_reduce_fusion
  96.7 1.7 copy.18
  98.4 1.6 constant_dynamic-slice_fusion
  100.0 0.7 reshape.115
  100.8 1.5 copy.19
  102.9 1.0 dynamic-slice_reduce_fusion.1
  104.6 0.7 copy-done.5
  105.3 1.1 bias.1
  106.4 4.3 %all-to-all-start.3 = ((f32[4,1,128]{2,1,0:T(1,128)}), f32[4,1,128]{2,1,0:T(1,128)S(1)}, u32[]{:S(2)}, u32[]{:S(2)}) async-start(f32[4,1,128]{2,1,0:T(1,128)} %get-tuple-element.28), calls=%async_computation.3 | async-start | bytes 4096 | tf_op jit(solution)/shard_map/all_to_all | solution.py:235
  110.7 0.9 copy-done.4
  111.6 9.7 %tiles.1 = bf16[2048,2048]{1,0:T(8,128)(2,1)} custom-call(bf16[128,768]{1,0:T(8,128)(2,1)S(1)} %copy-done.4, bf16[768,2048]{1,0:T(8,128)(2,1)S(1)} %bitcast.32), custom_call_target="tpu_custom_call" | custom-call | tf_op jit(solution)/shard_map/tiles/pallas_call | solution.py:151
  122.6 220.6 %all_to_all.26 = bf16[128,16,2048]{2,1,0:T(8,128)(2,1)S(1)} all-to-all(bf16[128,16,2048]{2,1,0:T(8,128)(2,1)} %bitcast.39), channel_id=1, replica_groups=mesh['build_0'=8,'build_1'=8,'build_2'=2,'prop'=4] {'build_0','build_1',..., dimensions={0} | all-to-all | bytes 16777216 | tf_op jit(solution)/shard_map/all_to_all | solution.py:240
  343.2 15.1 %series.1 = bf16[2048,128]{1,0:T(8,128)(2,1)} custom-call(bf16[2048,2048]{1,0:T(8,128)(2,1)S(1)} %bitcast.30, bf16[2048,128]{1,0:T(8,128)(2,1)} %bitcast.5.state_ref), custom_call_target="tpu_custom_call" | custom-call | tf_op jit(solution)/shard_map/series/pallas_call | solution.py:183
  (22 shorter events, 2.5 us)
Async XLA Ops:
  0.6 51.0 %copy-start = (bf16[48,16,128]{2,1,0:T(8,128)(2,1)S(1)}, bf16[48,16,128]{2,1,0:T(8,128)(2,1)}, u32[]{:S(2)}) copy-start(bf16[48,16,128]{2,1,0:T(8,128)(2,1)} %param.8) | copy-start | bytes 589828
  0.6 110.1 %copy-start.1 = (bf16[48,16,2048]{2,1,0:T(8,128)(2,1)S(1)}, bf16[48,16,2048]{2,1,0:T(8,128)(2,1)}, u32[]{:S(2)}) copy-start(bf16[48,16,2048]{2,1,0:T(8,128)(2,1)} %param.7) | copy-start | bytes 9437188
  0.7 1.2 copy-start.3
  1.8 0.8 copy-start.6
  2.6 97.4 %copy-start.8 = (f32[512]{0:T(512)S(1)}, f32[512]{0:T(512)}, u32[]{:S(2)}) copy-start(f32[512]{0:T(512)} %param.12) | copy-start | bytes 6148
  48.7 0.7 copy-start.7
  52.0 33.8 %all-to-all-start.1 = ((bf16[128,16,128]{2,1,0:T(8,128)(2,1)}), bf16[128,16,128]{2,1,0:T(8,128)(2,1)}, u32[]{:S(2)}, u32[]{:S(2)}) async-start(bf16[128,16,128]{2,1,0:T(8,128)(2,1)} %get-tuple-element.19), calls=%async_computation.1 | async-start | bytes 1048576 | tf_op jit(solution)/shard_map/all_to_all | solution.py:220
  85.8 1.0 copy-start.2
  87.5 17.1 %all-to-all-start.2 = ((f32[8,48,128]{2,1,0:T(8,128)}), f32[8,48,128]{2,1,0:T(8,128)S(1)}, u32[]{:S(2)}, u32[]{:S(2)}) async-start(f32[8,48,128]{2,1,0:T(8,128)} %merge.1), calls=%async_computation.2 | async-start | bytes 393216 | tf_op jit(solution)/shard_map/all_to_all | solution.py:226
  104.6 0.7 copy-start.5
  106.4 14.9 %all-to-all-start.3 = ((f32[4,1,128]{2,1,0:T(1,128)}), f32[4,1,128]{2,1,0:T(1,128)S(1)}, u32[]{:S(2)}, u32[]{:S(2)}) async-start(f32[4,1,128]{2,1,0:T(1,128)} %get-tuple-element.28), calls=%async_computation.3 | async-start | bytes 4096 | tf_op jit(solution)/shard_map/all_to_all | solution.py:235
  110.7 0.9 copy-start.4

commit v4 on v3

--- a/solution.py
+++ b/solution.py
@@ -14,10 +14,12 @@
 WHOLE = pl.BlockSpec(memory_space=pltpu.VMEM)
 
 
-def spread(value, axis):
-    count = lax.axis_size(axis)
-    copies = jnp.broadcast_to(value[None], (count, *value.shape))
-    return lax.all_to_all(copies, axis, split_axis=0, concat_axis=0, tiled=True)
+def in_hbm(value):
+    return pltpu.with_memory_space_constraint(value, pltpu.HBM)
+
+
+def whole_block(shape):
+    return pl.BlockSpec(shape, lambda i: (0,) * len(shape))
 
 
 def theta_kernel(state_ref, inverse_ref, out_ref):
@@ -33,12 +35,13 @@
     orbitals, electrons = state.shape
     return pl.pallas_call(
         theta_kernel,
-        in_specs=[WHOLE, WHOLE],
-        out_specs=WHOLE,
+        grid=(1,),
+        in_specs=[whole_block(state.shape), whole_block(inverse.shape)],
+        out_specs=whole_block((orbitals, 2 * electrons)),
         out_shape=jax.ShapeDtypeStruct((orbitals, 2 * electrons), state.dtype),
         compiler_params=pltpu.CompilerParams(vmem_limit_bytes=8 << 20),
         name="theta",
-    )(state, inverse)
+    )(in_hbm(state), in_hbm(inverse))
 
 
 def pick_kernel(prop_count, sources_ref, got_ref, theta_ref, starts_ref):
@@ -65,7 +68,7 @@
         out_shape=[jax.ShapeDtypeStruct(shape, got.dtype), pltpu.HBM(shape, got.dtype)],
         compiler_params=pltpu.CompilerParams(vmem_limit_bytes=8 << 20),
         name="pick",
-    )(sources, got)
+    )(in_hbm(sources), got)
 
 
 def merge_kernel(parts_ref, out_ref):
@@ -77,29 +80,46 @@
 def summed_copies(parts, copies):
     return pl.pallas_call(
         merge_kernel,
-        in_specs=[WHOLE],
-        out_specs=WHOLE,
+        grid=(1,),
+        in_specs=[whole_block(parts.shape)],
+        out_specs=whole_block((copies, *parts.shape[1:])),
         out_shape=pltpu.HBM((copies, *parts.shape[1:]), parts.dtype),
         compiler_params=pltpu.CompilerParams(vmem_limit_bytes=8 << 20),
         name="merge",
-    )(parts)
-
-
-def bias_kernel(rows, parts_ref, fields_ref, weights_ref, sources_ref, own_ref, wide_ref, sums_ref, kept_ref):
-    vectors, count = fields_ref.shape
+    )(in_hbm(parts))
+
+
+def bias_kernel(rows, parts_ref, fields_ref, weights_ref, sources_ref, wide_ref, sums_ref, kept_ref):
+    vectors, walkers = fields_ref.shape
+    count = parts_ref.shape[2]
     deep = wide_ref.shape[1]
     shift = rows.bit_length() - 1
+    stride = walkers // count
+    member = lax.axis_index("prop")
+    builder = lax.axis_index(BUILD[0])
+    for axis in BUILD[1:]:
+        builder = builder * lax.axis_size(axis) + lax.axis_index(axis)
+    exact = functools.partial(
+        jnp.dot, precision=lax.Precision.HIGHEST, preferred_element_type=jnp.float32
+    )
+    place = lax.broadcasted_iota(jnp.int32, (walkers, count), 0)
+    walker = lax.broadcasted_iota(jnp.int32, (walkers, count), 1)
+    select = (place == walker * stride + member).astype(jnp.float32)
+    fields = exact(fields_ref[...], select)
+    weights = exact(weights_ref[...], select)
+    sources = exact((sources_ref[...] // stride).astype(jnp.float32), select)
     bias = jnp.sum(parts_ref[...], axis=0)
-    fields = fields_ref[...]
     coeffs = (fields - bias).astype(jnp.bfloat16)
     exponent = jnp.sum(bias * (fields - 0.5 * bias), axis=0, keepdims=True)
-    grown = weights_ref[...] * jnp.exp(exponent)
-    kept = jnp.sum(grown * own_ref[...], axis=1, keepdims=True)
-    kept_ref[...] = jnp.broadcast_to(kept, kept_ref.shape)
+    grown = weights * jnp.exp(exponent)
+    lane = lax.broadcasted_iota(jnp.int32, (1, count), 1)
+    own = jnp.sum(jnp.where(lane == builder, sources, 0.0), axis=1, keepdims=True)
+    kept = jnp.where(lane.astype(jnp.float32) == own, grown, 0.0)
+    kept_ref[...] = jnp.broadcast_to(jnp.sum(kept, axis=1, keepdims=True), kept_ref.shape)
     total = jnp.sum(grown, axis=1, keepdims=True)
     sums_ref[...] = jnp.broadcast_to(total[None], sums_ref.shape)
-    walker = lax.broadcasted_iota(jnp.int32, (count, count), 0)
-    chosen = (walker == sources_ref[...]).astype(jnp.bfloat16)
+    row = lax.broadcasted_iota(jnp.int32, (count, count), 0).astype(jnp.float32)
+    chosen = (row == sources).astype(jnp.bfloat16)
     picked = jnp.dot(coeffs, chosen, preferred_element_type=jnp.float32).T
     group = lax.broadcasted_iota(jnp.int32, (vectors, deep), 1) >> shift
     vector = lax.broadcasted_iota(jnp.int32, (vectors, deep), 0)
@@ -109,20 +129,27 @@
     ).astype(jnp.bfloat16)
 
 
-def bias_and_weights(parts, fields, weights, sources, own, rows, prop_count):
-    vectors, count = fields.shape
+def bias_and_weights(parts, fields, weights, sources, rows, prop_count):
+    vectors = fields.shape[0]
+    count = parts.shape[2]
+    arrays = (parts, fields, weights, sources)
     return pl.pallas_call(
         functools.partial(bias_kernel, rows),
-        in_specs=[WHOLE] * 5,
-        out_specs=[WHOLE] * 3,
+        grid=(1,),
+        in_specs=[whole_block(array.shape) for array in arrays],
+        out_specs=[
+            whole_block((count, vectors * rows)),
+            whole_block((prop_count, 1, count)),
+            whole_block((1, count)),
+        ],
         out_shape=[
-            pltpu.HBM((count, vectors * rows), jnp.bfloat16),
-            pltpu.HBM((prop_count, 1, count), jnp.float32),
+            jax.ShapeDtypeStruct((count, vectors * rows), jnp.bfloat16),
+            jax.ShapeDtypeStruct((prop_count, 1, count), jnp.float32),
             jax.ShapeDtypeStruct((1, count), jnp.float32),
         ],
         compiler_params=pltpu.CompilerParams(vmem_limit_bytes=8 << 20),
         name="bias",
-    )(parts, fields, weights, sources, own)
+    )(*arrays)
 
 
 def tiles_kernel(rows, wide_ref, vectors_ref, out_ref):
@@ -130,13 +157,11 @@
     block = out_ref.shape[0]
     few = block // rows
     shift = rows.bit_length() - 1
-    step = pl.program_id(0)
     owner = lax.broadcasted_iota(jnp.int32, (block, few), 0) >> shift
     repeat = (owner == lax.broadcasted_iota(jnp.int32, (block, few), 1)).astype(jnp.bfloat16)
     row = lax.broadcasted_iota(jnp.int32, (block, deep), 0) & (rows - 1)
     column = lax.broadcasted_iota(jnp.int32, (block, deep), 1) & (rows - 1)
-    here = wide_ref[pl.ds(pl.multiple_of(step * few, few), few), :]
-    left = jnp.dot(repeat, here, preferred_element_type=jnp.float32)
+    left = jnp.dot(repeat, wide_ref[...], preferred_element_type=jnp.float32)
     left = jnp.where(row == column, left, 0.0).astype(jnp.bfloat16)
     out_ref[...] = jnp.dot(left, vectors_ref[...], preferred_element_type=jnp.float32).astype(
         out_ref.dtype
@@ -147,14 +172,14 @@
     vectors, rows, orbitals = cholesky.shape
     count = wide.shape[0]
     flat = cholesky.reshape(vectors * rows, orbitals)
-    block = 256
+    block = 512
     tiles = pl.pallas_call(
         functools.partial(tiles_kernel, rows),
         grid=(count * rows // block,),
-        in_specs=[WHOLE, WHOLE],
+        in_specs=[pl.BlockSpec((block // rows, vectors * rows), lambda i: (i, 0)), WHOLE],
         out_specs=pl.BlockSpec((block, orbitals), lambda i: (i, 0)),
         out_shape=pltpu.HBM((count * rows, orbitals), jnp.bfloat16),
-        compiler_params=pltpu.CompilerParams(vmem_limit_bytes=16 << 20),
+        compiler_params=pltpu.CompilerParams(vmem_limit_bytes=20 << 20),
         name="tiles",
     )(wide, flat)
     return tiles.reshape(count, rows, orbitals)
@@ -194,16 +219,9 @@
     )(potential, state)
 
 
-def of_group(values, member, build_count, prop_count):
-    split = values.reshape(build_count, prop_count, *values.shape[1:])
-    return lax.dynamic_index_in_dim(split, member, 1, False)
-
-
 def shards(cholesky, half_vectors, walkers, inverse_intersection, fields, weights, sources):
     build_count = lax.axis_size(BUILD)
     prop_count = lax.axis_size("prop")
-    builder = lax.axis_index(BUILD)
-    member = lax.axis_index("prop")
     orbitals = walkers.shape[1]
     electrons = walkers.shape[2]
     rows = orbitals // build_count
@@ -219,18 +237,11 @@
     starts, partial_bias = lax.optimization_barrier((starts, partial_bias))
     begin_state = send(starts).reshape(orbitals, electrons)
     line_parts = lax.all_gather(partial_bias, ("build_1", "build_2"))
-    begin_state, line_parts, fields, weights, sources = lax.optimization_barrier(
-        (begin_state, line_parts, fields, weights, sources)
-    )
+    begin_state, line_parts = lax.optimization_barrier((begin_state, line_parts))
     line_bias = summed_copies(line_parts, lax.axis_size("build_0"))
     parts = lax.all_to_all(line_bias, "build_0", split_axis=0, concat_axis=0, tiled=True)
-    group_fields = of_group(fields, member, build_count, prop_count).T
-    group_weights = of_group(weights, member, build_count, prop_count)[None]
-    group_sources = of_group(sources, member, build_count, prop_count) // prop_count
-    own_source = lax.dynamic_index_in_dim(group_sources, builder, 0, False)
-    own = (jnp.arange(build_count, dtype=jnp.int32) == own_source).astype(jnp.float32)
     wide, sums, kept = bias_and_weights(
-        parts, group_fields, group_weights, group_sources[None], own[None], rows, prop_count
+        parts, in_hbm(fields.T), in_hbm(weights[None]), in_hbm(sources[None]), rows, prop_count
     )
     sums = lax.all_to_all(sums, "prop", split_axis=0, concat_axis=0, tiled=True)
     tiles = potential_tiles(wide, cholesky)

time: 360 us -> 353 us (0.981)
  local copies, waits for them, and re-layouts: 14.9 us -> 0.01 us
  blocking collectives: 291 us -> 304 us
  starting transfers between devices: 20 us -> 13.3 us
    all_to_all x0 -> x1, blocking collectives: none -> 16.5 us  [shards(): lax.all_to_all(line_bias, 'build_0', split_axis=0, concat_axis=0, tiled=T...]
    all_to_all x1 -> x0, starting transfers between devices: 6.76 us -> none  [shards(): lax.all_to_all(line_bias, 'build_0', split_axis=0, concat_axis=0, tiled=T...]
    dynamic_slice x5 -> x0, local copies, waits for them, and re-layouts: 5.76 us -> none  [the longest x4 5.18 us: of_group(): return lax.dynamic_index_in_dim(split, member, 1, False)]
    unnamed x18 -> x4, local copies, waits for them, and re-layouts: 5.29 us -> 0.01 us
    all_to_all x1, blocking collectives: 221 us -> 216 us  [shards(): potential = send(tiles).reshape(orbitals, orbitals)]
  transfers between devices with their start and end apart: 3 -> 2, of which waited for: 0 -> 0; matrix products, arithmetic and copies ran while one was open for 3% -> 0% of each run, Pallas kernels for 3% -> 3%
where the time goes in v4:
time: 353 us; the launch traced here: 352 us
  blocking collectives  304 us (86%)
  Pallas kernels  32.1 us (9%)
  starting transfers between devices  13.3 us (4%)
    all_to_all x1, blocking collectives, shards(): potential = send(tiles).reshape(orbitals, orbitals)  216 us
    all_to_all x1, blocking collectives, shards(): got = send(outgoing.reshape(build_count, rows, 2 * electrons))  45.8 us
    all_gather x1, blocking collectives, shards(): line_parts = lax.all_gather(partial_bias, ('build_1', 'build_2'))  24.8 us
    all_to_all x1, blocking collectives, shards(): lax.all_to_all(line_bias, 'build_0', split_axis=0, concat_axis=0, tiled=T...  16.5 us
    pallas_call x1, Pallas kernels, series(): pl.pallas_call(series_kernel, in_specs=[WHOLE, WHOLE], out_specs=WHOLE, o...  15.1 us
    pallas_call x1, Pallas kernels, potential_tiles(): pl.pallas_call(functools.partial(tiles_kernel, rows), grid=(count * rows...  9.31 us
    all_to_all x1, starting transfers between devices, shards(): begin_state = send(starts).reshape(orbitals, electrons)  9.03 us
  transfers between devices with their start and end apart: 2, of which 0 were waited for; matrix products, arithmetic and copies ran while one was open for 0% of the time, Pallas kernels for 3%

profile of v4, /device:TPU:43, one launch (start us, length us, event | category | flops | bytes accessed | tf_op | source)
XLA Modules:
  0.0 352.4 jit_solution(11214087312760495679)
XLA Ops:
  0.6 0.0 copy-start
  0.6 0.0 copy-start.1
  0.7 1.5 theta.1
  2.2 45.8 %all_to_all.25.got_ref = bf16[128,16,256]{2,1,0:T(8,128)(2,1)S(1)} all-to-all(bf16[128,16,256]{2,1,0:T(8,128)(2,1)S(1)} %bitcast.20), channel_id=1, replica_groups=mesh['build_0'=8,'build_1'=8,'build_2'=2,'prop'=4] {'build_0','build_1',..., dimensions={0} | all-to-all | bytes 2097152 | tf_op jit(solution)/shard_map/all_to_all | solution.py:232
  48.0 2.4 pick.1
  50.3 0.0 copy-done
  50.4 0.3 convolution_bitcast_fusion
  50.7 9.0 %all-to-all-start.1 = ((bf16[128,16,128]{2,1,0:T(8,128)(2,1)}), bf16[128,16,128]{2,1,0:T(8,128)(2,1)}, u32[]{:S(2)}, u32[]{:S(2)}) async-start(bf16[128,16,128]{2,1,0:T(8,128)(2,1)} %get-tuple-element.16), calls=%async_computation.1 | async-start | bytes 1048576 | tf_op jit(solution)/shard_map/all_to_all | solution.py:238
  59.7 24.8 %all-gather = f32[768,128]{1,0:T(8,128)} all-gather(f32[48,128]{1,0:T(8,128)S(1)} %convolution_bitcast_fusion), channel_id=2, replica_groups=mesh['build_0'=8,'build_1'=8,'build_2'=2,'prop'=4] {'build_1','build_2'}, dimensions={0}, use_global_device_ids=true | all-gather | bytes 417792 | tf_op jit(solution)/shard_map/all_gather | solution.py:239
  84.4 0.0 all-to-all-done.1
  84.4 1.7 merge.1
  86.1 16.5 %all_to_all.26.parts_ref = f32[8,48,128]{2,1,0:T(8,128)S(1)} all-to-all(f32[8,48,128]{2,1,0:T(8,128)} %merge.1), channel_id=1, replica_groups=mesh['build_0'=8,'build_1'=8,'build_2'=2,'prop'=4] {'build_0'}, dimensions={0} | all-to-all | bytes 393216 | tf_op jit(solution)/shard_map/all_to_all | solution.py:242
  102.7 2.1 bias.1
  104.8 4.3 %all-to-all-start.3 = ((f32[4,1,128]{2,1,0:T(1,128)}), f32[4,1,128]{2,1,0:T(1,128)S(1)}, u32[]{:S(2)}, u32[]{:S(2)}) async-start(f32[4,1,128]{2,1,0:T(1,128)} %get-tuple-element.22), calls=%async_computation.3 | async-start | bytes 4096 | tf_op jit(solution)/shard_map/all_to_all | solution.py:246
  109.1 0.0 copy-done.1
  109.1 9.3 %tiles.1 = bf16[2048,2048]{1,0:T(8,128)(2,1)} custom-call(bf16[128,768]{1,0:T(8,128)(2,1)S(1)} %get-tuple-element.19.wide_ref, bf16[768,2048]{1,0:T(8,128)(2,1)S(1)} %bitcast.21), custom_call_target="tpu_custom_call" | custom-call | tf_op jit(solution)/shard_map/tiles/pallas_call | solution.py:176
  118.4 0.0 all-to-all-done.3
  118.4 0.6 slice_reduce_fusion
  119.7 216.4 %all_to_all.27 = bf16[128,16,2048]{2,1,0:T(8,128)(2,1)S(1)} all-to-all(bf16[128,16,2048]{2,1,0:T(8,128)(2,1)} %bitcast.23), channel_id=1, replica_groups=mesh['build_0'=8,'build_1'=8,'build_2'=2,'prop'=4] {'build_0','build_1',..., dimensions={0} | all-to-all | bytes 16777216 | tf_op jit(solution)/shard_map/all_to_all | solution.py:251
  336.1 15.1 %series.1 = bf16[2048,128]{1,0:T(8,128)(2,1)} custom-call(bf16[2048,2048]{1,0:T(8,128)(2,1)S(1)} %bitcast.19, bf16[2048,128]{1,0:T(8,128)(2,1)} %bitcast.5.state_ref), custom_call_target="tpu_custom_call" | custom-call | tf_op jit(solution)/shard_map/series/pallas_call | solution.py:208
Async XLA Ops:
  0.6 49.7 %copy-start = (bf16[48,16,128]{2,1,0:T(8,128)(2,1)S(1)}, bf16[48,16,128]{2,1,0:T(8,128)(2,1)}, u32[]{:S(2)}) copy-start(bf16[48,16,128]{2,1,0:T(8,128)(2,1)} %param.8) | copy-start | bytes 589828
  0.6 108.4 %copy-start.1 = (bf16[48,16,2048]{2,1,0:T(8,128)(2,1)S(1)}, bf16[48,16,2048]{2,1,0:T(8,128)(2,1)}, u32[]{:S(2)}) copy-start(bf16[48,16,2048]{2,1,0:T(8,128)(2,1)} %param.7) | copy-start | bytes 9437188
  50.7 33.8 %all-to-all-start.1 = ((bf16[128,16,128]{2,1,0:T(8,128)(2,1)}), bf16[128,16,128]{2,1,0:T(8,128)(2,1)}, u32[]{:S(2)}, u32[]{:S(2)}) async-start(bf16[128,16,128]{2,1,0:T(8,128)(2,1)} %get-tuple-element.16), calls=%async_computation.1 | async-start | bytes 1048576 | tf_op jit(solution)/shard_map/all_to_all | solution.py:238
  104.8 13.6 %all-to-all-start.3 = ((f32[4,1,128]{2,1,0:T(1,128)}), f32[4,1,128]{2,1,0:T(1,128)S(1)}, u32[]{:S(2)}, u32[]{:S(2)}) async-start(f32[4,1,128]{2,1,0:T(1,128)} %get-tuple-element.22), calls=%async_computation.3 | async-start | bytes 4096 | tf_op jit(solution)/shard_map/all_to_all | solution.py:246

commit v5 on v4

--- a/solution.py
+++ b/solution.py
@@ -185,9 +185,14 @@
     return tiles.reshape(count, rows, orbitals)
 
 
-def series_kernel(potential_ref, state_ref, out_ref, total_ref, term_ref):
+def series_kernel(
+    scale, potential_ref, state_ref, sums_ref, kept_ref, out_ref, weight_ref, total_ref, term_ref
+):
+    overall = jnp.sum(sums_ref[...], axis=0)
+    weight = kept_ref[...] * scale / overall
+    weight_ref[...] = weight[0, :1]
     orbitals = potential_ref.shape[0]
-    block = 256
+    block = 512
     for degree in range(1, ORDER + 1):
         source = state_ref if degree == 1 else term_ref.at[(degree - 1) % 2]
         held = source[...]
@@ -203,20 +208,23 @@
                 term_ref[degree % 2, here, :] = product.astype(jnp.bfloat16)
 
 
-def series(potential, state):
+def series(potential, state, sums, kept, scale):
     orbitals, electrons = state.shape
     return pl.pallas_call(
-        series_kernel,
-        in_specs=[WHOLE, WHOLE],
-        out_specs=WHOLE,
-        out_shape=jax.ShapeDtypeStruct((orbitals, electrons), jnp.bfloat16),
+        functools.partial(series_kernel, scale),
+        in_specs=[WHOLE] * 4,
+        out_specs=[WHOLE] * 2,
+        out_shape=[
+            jax.ShapeDtypeStruct((orbitals, electrons), jnp.bfloat16),
+            jax.ShapeDtypeStruct((1,), jnp.float32),
+        ],
         scratch_shapes=[
             pltpu.VMEM((orbitals, electrons), jnp.float32),
             pltpu.VMEM((2, orbitals, electrons), jnp.bfloat16),
         ],
         compiler_params=pltpu.CompilerParams(vmem_limit_bytes=16 << 20),
         name="series",
-    )(potential, state)
+    )(potential, in_hbm(state), in_hbm(sums), in_hbm(kept))
 
 
 def shards(cholesky, half_vectors, walkers, inverse_intersection, fields, weights, sources):
@@ -234,23 +242,23 @@
     partial_bias = jnp.einsum(
         "wri,gri->gw", got_theta, half_vectors, preferred_element_type=jnp.float32
     )
-    starts, partial_bias = lax.optimization_barrier((starts, partial_bias))
+    exchange = functools.partial(lax.all_to_all, split_axis=0, concat_axis=0, tiled=True)
+    chip_parts = lax.all_gather(partial_bias, "build_2")
+    chip_bias = summed_copies(chip_parts, lax.axis_size("build_1"))
+    line_bias = summed_copies(exchange(chip_bias, "build_1"), lax.axis_size("build_0"))
+    parts = exchange(line_bias, "build_0")
+    starts, parts = lax.optimization_barrier((starts, parts))
     begin_state = send(starts).reshape(orbitals, electrons)
-    line_parts = lax.all_gather(partial_bias, ("build_1", "build_2"))
-    begin_state, line_parts = lax.optimization_barrier((begin_state, line_parts))
-    line_bias = summed_copies(line_parts, lax.axis_size("build_0"))
-    parts = lax.all_to_all(line_bias, "build_0", split_axis=0, concat_axis=0, tiled=True)
     wide, sums, kept = bias_and_weights(
-        parts, in_hbm(fields.T), in_hbm(weights[None]), in_hbm(sources[None]), rows, prop_count
-    )
-    sums = lax.all_to_all(sums, "prop", split_axis=0, concat_axis=0, tiled=True)
+        parts, in_hbm(fields.T), in_hbm(weights[None]), in_hbm(sources[None]), rows, 1
+    )
+    sums = lax.all_gather(sums[0], "prop")
     tiles = potential_tiles(wide, cholesky)
-    overall = jnp.sum(sums[:, 0, :1], axis=0)
-    new_weight = kept[0, :1] * (build_count * prop_count) / overall
-    tiles, begin_state, new_weight = lax.optimization_barrier((tiles, begin_state, new_weight))
+    tiles, begin_state, sums, kept = lax.optimization_barrier((tiles, begin_state, sums, kept))
     potential = send(tiles).reshape(orbitals, orbitals)
     potential = pltpu.with_memory_space_constraint(potential, pltpu.VMEM)
-    stepped = series(potential, begin_state)
+    scale = float(build_count * prop_count)
+    stepped, new_weight = series(potential, begin_state, sums, kept, scale)
     return (stepped[None], new_weight)
 
 

time: 353 us -> 350 us (level)
  the two profiles are of different devices: /device:TPU:43 before, /device:TPU:32 now
where the time goes in v5:
time: 350 us; the launch traced here: 349 us
  blocking collectives  303 us (87%)
  Pallas kernels  33 us (9%)
  starting transfers between devices  12.2 us (3%)
    all_to_all x1, blocking collectives, shards(): potential = send(tiles).reshape(orbitals, orbitals)  219 us
    all_to_all x1, blocking collectives, shards(): got = send(outgoing.reshape(build_count, rows, 2 * electrons))  44.9 us
    pallas_call x1, Pallas kernels, series(): pl.pallas_call(functools.partial(series_kernel, scale), in_specs=[WHOLE]...  15 us
    all_to_all x1, blocking collectives, shards(): parts = exchange(line_bias, 'build_0')  13.6 us
    all_to_all x1, blocking collectives, shards(): exchange(chip_bias, 'build_1')  13 us
    all_to_all x1, starting transfers between devices, shards(): begin_state = send(starts).reshape(orbitals, electrons)  12.2 us
    all_gather x1, blocking collectives, shards(): sums = lax.all_gather(sums[0], 'prop')  9.68 us
    pallas_call x1, Pallas kernels, potential_tiles(): pl.pallas_call(functools.partial(tiles_kernel, rows), grid=(count * rows...  9.3 us
  transfers between devices with their start and end apart: 1, of which 0 were waited for; matrix products, arithmetic and copies ran while one was open for 0% of the time, Pallas kernels for 3%

profile of v5, /device:TPU:32, one launch (start us, length us, event | category | flops | bytes accessed | tf_op | source)
XLA Modules:
  0.0 349.4 jit_solution(10214743660469460848)
XLA Ops:
  0.6 0.0 copy-start
  0.6 0.0 copy-start.1
  0.7 1.5 theta.1
  2.2 44.9 %all_to_all.25.got_ref = bf16[128,16,256]{2,1,0:T(8,128)(2,1)S(1)} all-to-all(bf16[128,16,256]{2,1,0:T(8,128)(2,1)S(1)} %bitcast.17), channel_id=1, replica_groups=mesh['build_0'=8,'build_1'=8,'build_2'=2,'prop'=4] {'build_0','build_1',..., dimensions={0} | all-to-all | bytes 2097152 | tf_op jit(solution)/shard_map/all_to_all | solution.py:240
  47.0 2.4 pick.1
  49.4 0.0 copy-done
  49.4 0.3 convolution_bitcast_fusion
  49.7 2.0 all-gather
  51.7 1.5 merge.2
  53.2 13.0 %all_to_all.26.parts_ref = f32[8,48,128]{2,1,0:T(8,128)} all-to-all(f32[8,48,128]{2,1,0:T(8,128)} %merge.2), channel_id=1, replica_groups=mesh['build_0'=8,'build_1'=8,'build_2'=2,'prop'=4] {'build_1'}, dimensions={0} | all-to-all | bytes 393216 | tf_op jit(solution)/shard_map/all_to_all | solution.py:248
  66.1 1.6 merge.3
  67.8 13.6 %all_to_all.27.parts_ref = f32[8,48,128]{2,1,0:T(8,128)S(1)} all-to-all(f32[8,48,128]{2,1,0:T(8,128)} %merge.3), channel_id=1, replica_groups=mesh['build_0'=8,'build_1'=8,'build_2'=2,'prop'=4] {'build_0'}, dimensions={0} | all-to-all | bytes 393216 | tf_op jit(solution)/shard_map/all_to_all | solution.py:249
  81.4 12.2 %all-to-all-start.3 = ((bf16[128,16,128]{2,1,0:T(8,128)(2,1)}), bf16[128,16,128]{2,1,0:T(8,128)(2,1)}, u32[]{:S(2)}, u32[]{:S(2)}) async-start(bf16[128,16,128]{2,1,0:T(8,128)(2,1)} %get-tuple-element.19), calls=%async_computation.3 | async-start | bytes 1048576 | tf_op jit(solution)/shard_map/all_to_all | solution.py:251
  93.6 1.8 bias.1
  95.4 0.0 copy-start.2
  95.4 0.5 copy-done.2
  95.9 0.0 copy-done.1
  95.9 9.3 %tiles.1 = bf16[2048,2048]{1,0:T(8,128)(2,1)} custom-call(bf16[128,768]{1,0:T(8,128)(2,1)S(1)} %get-tuple-element.18.wide_ref, bf16[768,2048]{1,0:T(8,128)(2,1)S(1)} %bitcast.18), custom_call_target="tpu_custom_call" | custom-call | tf_op jit(solution)/shard_map/tiles/pallas_call | solution.py:176
  105.2 9.7 %all_gather.11.sums_ref = f32[4,1,128]{2,1,0:T(1,128)} all-gather(f32[1,1,128]{2,1,0:T(1,128)S(1)} %get-tuple-element.20), channel_id=1, replica_groups=mesh['build_0'=8,'build_1'=8,'build_2'=2,'prop'=4] {'prop'}, dimensions={0}, use_global_device_ids=true | all-gather | bytes 2560 | tf_op jit(solution)/shard_map/all_gather | solution.py:255
  114.9 0.0 all-to-all-done.3
  114.9 219.5 %all_to_all.28 = bf16[128,16,2048]{2,1,0:T(8,128)(2,1)S(1)} all-to-all(bf16[128,16,2048]{2,1,0:T(8,128)(2,1)} %bitcast.19), channel_id=1, replica_groups=mesh['build_0'=8,'build_1'=8,'build_2'=2,'prop'=4] {'build_0','build_1',..., dimensions={0} | all-to-all | bytes 16777216 | tf_op jit(solution)/shard_map/all_to_all | solution.py:258
  334.4 15.0 %series.1 = (bf16[2048,128]{1,0:T(8,128)(2,1)}, f32[1]{0:T(128)}) custom-call(bf16[2048,2048]{1,0:T(8,128)(2,1)S(1)} %bitcast.16, bf16[2048,128]{1,0:T(8,128)(2,1)} %bitcast.11.state_ref, f32[4,1,128]{2,1,0:T(1,128)} %all_gather.11.sums_ref, f32[1,128]{1,0:T(1,128)} %copy-done.2), custom_call_target="tpu_custom_call" | custom-call | tf_op jit(solution)/shard_map/series/pallas_call | solution.py:213
Async XLA Ops:
  0.6 48.8 %copy-start = (bf16[48,16,128]{2,1,0:T(8,128)(2,1)S(1)}, bf16[48,16,128]{2,1,0:T(8,128)(2,1)}, u32[]{:S(2)}) copy-start(bf16[48,16,128]{2,1,0:T(8,128)(2,1)} %param.8) | copy-start | bytes 589828
  0.6 95.3 %copy-start.1 = (bf16[48,16,2048]{2,1,0:T(8,128)(2,1)S(1)}, bf16[48,16,2048]{2,1,0:T(8,128)(2,1)}, u32[]{:S(2)}) copy-start(bf16[48,16,2048]{2,1,0:T(8,128)(2,1)} %param.7) | copy-start | bytes 9437188
  81.4 33.5 %all-to-all-start.3 = ((bf16[128,16,128]{2,1,0:T(8,128)(2,1)}), bf16[128,16,128]{2,1,0:T(8,128)(2,1)}, u32[]{:S(2)}, u32[]{:S(2)}) async-start(bf16[128,16,128]{2,1,0:T(8,128)(2,1)} %get-tuple-element.19), calls=%async_computation.3 | async-start | bytes 1048576 | tf_op jit(solution)/shard_map/all_to_all | solution.py:251
  95.4 0.5 copy-start.2
